TPU v7x, 512 devices: a whole 4x8x8 slice. The times are simulated.
512 devices in a mesh: dp: 8 (over z), dom: 64 (over y, x, core).
Axes of the slice: x: 4, y: 8, z: 8, core: 2. Of those that a mesh axis runs over, the one named last changes fastest.
Arguments:
- features: bfloat16 [8, 65536, 256], P('dp', 'dom'), may hold values from -6 to 6
- send_order: int32 [64, 1024], P('dom'), may hold values from 0 to 1023, each once within a row
- adj_count: int32 [512], P('dom'), may hold values from 2 to 4, as said below
- adj_target: int32 [512, 4], P('dom'), may hold values from 6 to 17, as said below
- adj_vals: bfloat16 [512, 4, 128, 128], P('dom'), may hold values from -0.3125 to 0.3125
- w_edge: bfloat16 [256, 256], replicated, may hold values from -0.375 to 0.375
- w_node: bfloat16 [512, 256], replicated, may hold values from -0.25 to 0.25
- cotangent: bfloat16 [8, 65536, 256], P('dp', 'dom'), may hold values from -6 to 6
Outputs:
- node_out: bfloat16 [8, 65536, 256], P('dp', 'dom')
- grad_features: bfloat16 [8, 65536, 256], P('dp', 'dom')
- grad_edge: float32 [256, 256], replicated
- grad_node: float32 [512, 256], replicated
Inputs may be any that keep to these rules, and one draw needn't show every extreme that they name: Each row of send_order is a permutation of 0 to 1023. `adj_count`: every partition has its own most count, reached by one of its blocks; some partition's most is 4. `adj_target`: targets lie in the own partition's blocks or in the last 2 blocks of the previous partition or the first 2 blocks of the next one; slot 0 of each partition's first column block targets the previous partition, and slot 1 of its last column block targets the next one.
All inputs are finite; a program needn't handle non-finite values.
Results may differ from a plain program's by a relative error of at most 0.009.
Values may be sent and summed in bfloat16 or wider, within the bound.
A program may use at most 64 MiB of HBM per device.

v0:
```python
import math

import jax
import jax.numpy as jnp
from jax import lax
from jax.sharding import PartitionSpec as P

RIM = 2


def passed_along(x, axis, by):
    peers = lax.axis_size(axis)
    return lax.ppermute(x, axis, [(i, (i + by) % peers) for i in range(peers)])


def split_up(x, dim, peers):
    dims = x.shape
    tiles = x.reshape(*dims[:dim], peers, dims[dim] // peers, *dims[dim + 1 :])
    return jnp.moveaxis(tiles, dim, 0)


def summed_on_arrival(x, axis, dim):
    peers = lax.axis_size(axis)
    tiles = lax.all_to_all(split_up(x, dim, peers), axis, 0, 0, tiled=True)
    return jnp.sum(tiles, axis=0)


def from_everyone(x, axis):
    peers = lax.axis_size(axis)
    return lax.all_to_all(jnp.broadcast_to(x[None], (peers, *x.shape)), axis, 0, 0, tiled=True)


def over_copies(x, axis):
    return from_everyone(x, axis).sum(axis=0)


def joined_along(tiles, dim):
    dims = list(tiles.shape[1:])
    dims[dim] *= tiles.shape[0]
    return jnp.moveaxis(tiles, 0, dim).reshape(dims)


def collect(x, axis, dim):
    return joined_along(from_everyone(x, axis), dim)


def dsilu(value):
    sig = jax.nn.sigmoid(value)
    return sig * (1.0 + value * (1.0 - sig))


def shards(features, send_order, adj_count, adj_target, adj_vals, w_edge, w_node, cotangent):
    ndom = lax.axis_size("dom")
    rows = features.shape[1]
    width = features.shape[2]
    per_peer = rows // ndom
    blocks = rows // 128
    slots = adj_target.shape[1]
    border = RIM
    order = send_order[0]
    picked = jnp.take(features[0], order, axis=0).reshape(ndom, per_peer, width)
    nodes = lax.all_to_all(picked, "dom", split_axis=0, concat_axis=0, tiled=True).reshape(
        rows, width
    )
    pre_edge = jnp.dot(nodes, w_edge, preferred_element_type=jnp.float32)
    message = jax.nn.silu(pre_edge).astype(jnp.bfloat16)
    msg_blocks = message.reshape(blocks, 128, width)
    wins = jnp.arange(3 * blocks, dtype=jnp.int32)
    live = jnp.arange(slots, dtype=jnp.int32)[None, :] < adj_count[:, None]
    table = (adj_target[None, :, :] == wins[:, None, None]) & live[None]
    table_f = table.astype(jnp.float32)
    table_b = table.astype(jnp.bfloat16)
    contrib = jnp.einsum("csrk,ckh->csrh", adj_vals, msg_blocks, preferred_element_type=jnp.float32)
    window = jnp.einsum("wcs,csrh->wrh", table_f, contrib, precision=lax.Precision.HIGHEST)
    window_b = window.astype(jnp.bfloat16)
    lead_pad = ((blocks - border, 0), (0, 0), (0, 0))
    tail_pad = ((0, blocks - border), (0, 0), (0, 0))
    send_prev = window_b[blocks - border : blocks]
    send_next = window_b[2 * blocks : 2 * blocks + border]
    from_next = passed_along(send_prev, "dom", -1)
    from_prev = passed_along(send_next, "dom", 1)
    from_next = jnp.pad(from_next, lead_pad)
    from_prev = jnp.pad(from_prev, tail_pad)
    agg = (
        window_b[blocks : 2 * blocks].astype(jnp.float32)
        + from_next.astype(jnp.float32)
        + from_prev.astype(jnp.float32)
    )
    aggregate = agg.astype(jnp.bfloat16).reshape(rows, width)
    joined = jnp.concatenate([nodes, aggregate], axis=1)
    pre_node = jnp.dot(joined, w_node, preferred_element_type=jnp.float32)
    node_out = (nodes.astype(jnp.float32) + jax.nn.silu(pre_node)).astype(jnp.bfloat16)
    gout = cotangent[0].astype(jnp.float32)
    d_node = (gout * dsilu(pre_node)).astype(jnp.bfloat16)
    back = jnp.einsum("nh,dh->nd", d_node, w_node, preferred_element_type=jnp.float32)
    d_nodes1 = gout + back[:, :width]
    d_agg = back[:, width:].astype(jnp.bfloat16).reshape(blocks, 128, width)
    give_next = d_agg[blocks - border :]
    give_prev = d_agg[:border]
    prev_rows = passed_along(give_next, "dom", 1)
    next_rows = passed_along(give_prev, "dom", -1)
    prev_rows = jnp.pad(prev_rows, lead_pad)
    next_rows = jnp.pad(next_rows, tail_pad)
    window_g = jnp.concatenate([prev_rows, d_agg, next_rows], axis=0)
    gathered = jnp.einsum(
        "wcs,wrh->csrh", table_b, window_g, preferred_element_type=jnp.float32
    ).astype(jnp.bfloat16)
    d_message = jnp.einsum("csrk,csrh->ckh", adj_vals, gathered, preferred_element_type=jnp.float32)
    d_message = d_message.astype(jnp.bfloat16).reshape(rows, width)
    d_edge = (d_message.astype(jnp.float32) * dsilu(pre_edge)).astype(jnp.bfloat16)
    d_nodes = (
        d_nodes1 + jnp.einsum("nh,dh->nd", d_edge, w_edge, preferred_element_type=jnp.float32)
    ).astype(jnp.bfloat16)
    returned = lax.all_to_all(
        d_nodes.reshape(ndom, per_peer, width), "dom", split_axis=0, concat_axis=0, tiled=True
    ).reshape(rows, width)
    grad_brick = jnp.zeros_like(returned).at[order].set(returned)
    local_edge = jnp.einsum("nd,nh->dh", nodes, d_edge, preferred_element_type=jnp.float32)
    local_node = jnp.einsum("nd,nh->dh", joined, d_node, preferred_element_type=jnp.float32)
    scale = 1.0 / math.sqrt(float(lax.axis_size("dp") * rows * ndom))
    stacked = jnp.concatenate([local_edge, local_node], axis=0)
    share = summed_on_arrival(stacked, "dom", 0)
    share = over_copies(share, "dp")
    whole = collect(share, "dom", 0)
    grad_edge = whole[:width]
    grad_node = whole[width:]
    return (node_out[None], grad_brick[None], grad_edge * scale, grad_node * scale)


def solution(mesh):
    in_specs = (
        P("dp", "dom", None),
        P("dom", None),
        P("dom"),
        P("dom", None),
        P("dom", None, None, None),
        P(),
        P(),
        P("dp", "dom", None),
    )
    out_specs = (P("dp", "dom", None), P("dp", "dom", None), P(), P())
    return jax.shard_map(shards, mesh=mesh, in_specs=in_specs, out_specs=out_specs, check_vma=False)
```

profile of v0, /device:TPU:1, one launch (start us, length us, event | category | flops | bytes accessed | tf_op | source)
XLA Modules:
  0.0 200.8 jit_solution(11974714847964144588)
XLA Ops:
  0.6 0.8 compare_select_fusion.1
  1.4 0.5 broadcast.79
  1.9 1.3 reduce.3
  3.3 0.1 squeeze.9
  3.4 4.6 %gather_fusion = bf16[1024,256]{1,0:T(8,128)(2,1)S(1)} fusion(bf16[1024,256]{1,0:T(8,128)(2,1)} %bitcast.67, s32[1024]{0:T(1024)S(1)} %broadcast_clamp_fusion), kind=kCustom, calls=%fused_computation | custom fusion | bytes 1052672 | tf_op jit(solution)/shard_map/jit(_take)/gather | solution.py:61
  8.0 1.0 broadcast_select_fusion
  9.0 11.6 %all-to-all-start = ((bf16[64,16,256]{2,1,0:T(8,128)(2,1)}), bf16[64,16,256]{2,1,0:T(8,128)(2,1)S(1)}, u32[]{:S(2)}, u32[]{:S(2)}) async-start(bf16[64,16,256]{2,1,0:T(8,128)(2,1)} %broadcast_select_fusion), calls=%async_computation | async-start | bytes 1048576 | tf_op jit(solution)/shard_map/all_to_all | solution.py:62
  20.7 17.7 %all-to-all-done = bf16[64,16,256]{2,1,0:T(8,128)(2,1)S(1)} async-done(((bf16[64,16,256]{2,1,0:T(8,128)(2,1)}), bf16[64,16,256]{2,1,0:T(8,128)(2,1)S(1)}, u32[]{:S(2)}, u32[]{:S(2)}) %all-to-all-start) | async-done | bytes 524320 | tf_op jit(solution)/shard_map/all_to_all | solution.py:62
  38.3 0.4 multiply_convert_fusion
  38.8 2.7 %convolution_bitcast_fusion = f32[8,4,128,256]{2,3,1,0:T(8,128)} fusion(bf16[8,128,256,1]{2,1,3,0:T(8,128)(2,1)S(1)} %bitcast.80, bf16[8,4,128,128]{3,2,1,0:T(8,128)(2,1)S(1)} %copy-done), kind=kOutput, calls=%fused_computation.7 | convolution fusion | flops 268435456 | bytes 5767168 | tf_op jit(solution)/shard_map/csrk,ckh->csrh/dot_general | solution.py:73
  41.5 5.5 %copy.25 = f32[8,4,128,256]{3,0,1,2:T(8,128)} copy(f32[8,4,128,256]{2,3,1,0:T(8,128)} %convolution_bitcast_fusion) | data formatting | bytes 8388608 | tf_op jit(solution)/shard_map/csrk,ckh->csrh/dot_general | solution.py:73
  47.0 4.2 %bitcast_convert_fusion = bf16[24,128,256]{2,0,1:T(8,128)(2,1)S(1)} fusion(f32[8,4,128,256]{3,0,1,2:T(8,128)} %copy.25, s32[8,4]{0,1:T(4,128)S(1)} %copy-done.5, pred[8,4]{0,1:T(4,128)(4,1)S(1)} %iota_compare_fusion.3), kind=kOutput, calls=%fused_computation.4 | convolution fusion | flops 302777856 | bytes 5767328 | tf_op jit(solution)/shard_map/wcs,csrh->wrh/dot_general | solution.py:74
  51.2 0.2 fusion.47
  51.4 2.3 %collective-permute-start = (bf16[2,128,256]{2,0,1:T(2,128)(2,1)S(1)}, bf16[2,128,256]{2,0,1:T(2,128)(2,1)S(1)}, u32[]{:S(2)}, u32[]{:S(2)}) collective-permute-start(bf16[2,128,256]{2,0,1:T(2,128)(2,1)S(1)} %get-tuple-element.4), channel_id=1, source_target_pairs={{0,63},{1,0},{2,1},{3,2},{4,3},{5,4},{6,5},{7,6},{8,7},{9,8},{10,9... | collective-permute-start | bytes 393224 | tf_op jit(solution)/shard_map/ppermute | solution.py:13
  53.7 3.3 %collective-permute-start.1 = (bf16[2,128,256]{2,0,1:T(2,128)(2,1)S(1)}, bf16[2,128,256]{2,0,1:T(2,128)(2,1)S(1)}, u32[]{:S(2)}, u32[]{:S(2)}) collective-permute-start(bf16[2,128,256]{2,0,1:T(2,128)(2,1)S(1)} %get-tuple-element.5), channel_id=1, source_target_pairs={{0,1},{1,2},{2,3},{3,4},{4,5},{5,6},{6,7},{7,8},{8,9},{9,10},{10,1... | collective-permute-start | bytes 393224 | tf_op jit(solution)/shard_map/ppermute | solution.py:13
  57.0 0.7 collective-permute-done
  57.7 1.2 collective-permute-done.1
  58.9 0.3 add_convert_fusion.1
  59.3 0.1 copy.26
  59.4 1.5 fusion.24
  60.9 1.8 fusion.49
  62.8 0.1 copy.27
  62.9 4.4 %collective-permute-start.2 = (bf16[2,128,256]{2,0,1:T(2,128)(2,1)S(1)}, bf16[2,128,256]{2,0,1:T(2,128)(2,1)S(1)}, u32[]{:S(2)}, u32[]{:S(2)}) collective-permute-start(bf16[2,128,256]{2,0,1:T(2,128)(2,1)S(1)} %copy.27), channel_id=1, source_target_pairs={{0,1},{1,2},{2,3},{3,4},{4,5},{5,6},{6,7},{7,8},{8,9},{9,10},{10,1... | collective-permute-start | bytes 393224 | tf_op jit(solution)/shard_map/ppermute | solution.py:13
  67.3 0.1 copy.28
  67.4 5.7 %collective-permute-start.3 = (bf16[2,128,256]{2,0,1:T(2,128)(2,1)S(1)}, bf16[2,128,256]{2,0,1:T(2,128)(2,1)S(1)}, u32[]{:S(2)}, u32[]{:S(2)}) collective-permute-start(bf16[2,128,256]{2,0,1:T(2,128)(2,1)S(1)} %copy.28), channel_id=1, source_target_pairs={{0,63},{1,0},{2,1},{3,2},{4,3},{5,4},{6,5},{7,6},{8,7},{9,8},{10,9... | collective-permute-start | bytes 393224 | tf_op jit(solution)/shard_map/ppermute | solution.py:13
  73.1 0.3 copy.29
  73.4 0.5 fusion.27
  73.9 0.2 collective-permute-done.3
  74.1 0.8 convolution_convert_fusion
  74.9 0.8 fusion.21
  75.7 0.4 fusion.25
  76.1 0.3 fusion.50
  76.5 0.1 reshape.107
  76.6 42.1 %all_to_all.25 = f32[64,12,256]{2,1,0:T(8,128)} all-to-all(f32[64,12,256]{2,1,0:T(8,128)S(1)} %reshape.107), channel_id=1, replica_groups=mesh['dp'=8,'dom'=64] {'dom'}, dimensions={0} | all-to-all | bytes 1572864 | tf_op jit(solution)/shard_map/all_to_all | solution.py:24
  118.8 1.3 reduce_sum.18
  120.1 0.7 broadcast_in_dim.42
  120.8 10.0 %all-to-all-start.3 = ((f32[8,12,256]{2,1,0:T(8,128)}), f32[8,12,256]{2,1,0:T(8,128)S(1)}, u32[]{:S(2)}, u32[]{:S(2)}) async-start(f32[8,12,256]{2,1,0:T(8,128)} %broadcast_in_dim.42), calls=%async_computation.3 | async-start | bytes 262144 | tf_op jit(solution)/shard_map/all_to_all | solution.py:30
  130.8 2.3 %fusion.17 = bf16[1024,256]{1,0:T(8,128)(2,1)} fusion(bf16[1024,256]{1,0:T(8,128)(2,1)S(1)} %fusion.25, bf16[256,256]{1,0:T(8,128)(2,1)S(1)} %copy-done.4, f32[1024,512]{1,0:T(8,128)} %get-tuple-element.13, bf16[1,1024,256]{2,1,0:T(8,128)(2,1)S(1)} %copy-done.2), kind=kOutput, calls=%fused_computation.23 | convolution fusion | flops 135266304 | bytes 2752512 | tf_op jit(solution)/shard_map/nh,dh->nd/dot_general | solution.py:112
  133.1 5.6 %all-to-all-done.3 = f32[8,12,256]{2,1,0:T(8,128)S(1)} async-done(((f32[8,12,256]{2,1,0:T(8,128)}), f32[8,12,256]{2,1,0:T(8,128)S(1)}, u32[]{:S(2)}, u32[]{:S(2)}) %all-to-all-start.3) | async-done | bytes 98336 | tf_op jit(solution)/shard_map/all_to_all | solution.py:30
  138.7 7.9 %all-to-all-start.1 = ((bf16[64,16,256]{2,1,0:T(8,128)(2,1)}), bf16[64,16,256]{2,1,0:T(8,128)(2,1)S(1)}, u32[]{:S(2)}, u32[]{:S(2)}) async-start(bf16[64,16,256]{2,1,0:T(8,128)(2,1)} %bitcast.24), calls=%async_computation.1 | async-start | bytes 1048576 | tf_op jit(solution)/shard_map/all_to_all | solution.py:114
  146.6 17.7 %all-to-all-done.1 = bf16[64,16,256]{2,1,0:T(8,128)(2,1)S(1)} async-done(((bf16[64,16,256]{2,1,0:T(8,128)(2,1)}), bf16[64,16,256]{2,1,0:T(8,128)(2,1)S(1)}, u32[]{:S(2)}, u32[]{:S(2)}) %all-to-all-start.1) | async-done | bytes 524320 | tf_op jit(solution)/shard_map/all_to_all | solution.py:114
  164.3 1.1 broadcast_in_dim.43
  165.4 5.7 %all-to-all-start.4 = ((f32[64,12,256]{2,1,0:T(8,128)}), f32[64,12,256]{2,1,0:T(8,128)S(1)}, u32[]{:S(2)}, u32[]{:S(2)}) async-start(f32[64,12,256]{2,1,0:T(8,128)} %broadcast_in_dim.43), calls=%async_computation.4 | async-start | bytes 2097152 | tf_op jit(solution)/shard_map/all_to_all | solution.py:30
  171.2 5.7 %scatter_custom_fusion = bf16[1024,256]{1,0:T(8,128)(2,1)} fusion(s32[1024]{0:T(1024)S(1)} %bitcast.82, bf16[1024,256]{1,0:T(8,128)(2,1)S(1)} %bitcast.77, bf16[]{:T(256)} %constant.20.clone.1), kind=kCustom, calls=%fused_computation.43 | custom fusion | bytes 524290 | tf_op jit(solution)/shard_map/scatter | solution.py:117
  176.9 22.3 %all-to-all-done.4 = f32[64,12,256]{2,1,0:T(8,128)S(1)} async-done(((f32[64,12,256]{2,1,0:T(8,128)}), f32[64,12,256]{2,1,0:T(8,128)S(1)}, u32[]{:S(2)}, u32[]{:S(2)}) %all-to-all-start.4) | async-done | bytes 786464 | tf_op jit(solution)/shard_map/all_to_all | solution.py:30
  199.2 0.1 reshape.108
  199.2 0.8 slice_multiply_fusion
  200.1 0.7 slice_multiply_fusion.1
  (22 shorter events, 0.2 us)
Async XLA Ops:
  0.6 38.2 %copy-start = (bf16[8,4,128,128]{3,2,1,0:T(8,128)(2,1)S(1)}, bf16[8,4,128,128]{3,2,1,0:T(8,128)(2,1)}, u32[]{:S(2)}) copy-start(bf16[8,4,128,128]{3,2,1,0:T(8,128)(2,1)} %param.12) | copy-start | bytes 3145732
  8.0 12.7 %copy-start.6 = (s32[8]{0:T(128)S(1)}, s32[8]{0:T(128)}, u32[]{:S(2)}) copy-start(s32[8]{0:T(128)} %param.10) | copy-start | bytes 100
  8.0 30.4 %copy-start.4 = (bf16[256,256]{1,0:T(8,128)(2,1)S(1)}, bf16[256,256]{1,0:T(8,128)(2,1)}, u32[]{:S(2)}) copy-start(bf16[256,256]{1,0:T(8,128)(2,1)} %param.13) | copy-start | bytes 393220
  9.0 29.3 %all-to-all-start = ((bf16[64,16,256]{2,1,0:T(8,128)(2,1)}), bf16[64,16,256]{2,1,0:T(8,128)(2,1)S(1)}, u32[]{:S(2)}, u32[]{:S(2)}) async-start(bf16[64,16,256]{2,1,0:T(8,128)(2,1)} %broadcast_select_fusion), calls=%async_computation | async-start | bytes 1048576 | tf_op jit(solution)/shard_map/all_to_all | solution.py:62
  41.5 5.5 %copy-start.5 = (s32[8,4]{0,1:T(4,128)S(1)}, s32[8,4]{0,1:T(4,128)}, u32[]{:S(2)}) copy-start(s32[8,4]{0,1:T(4,128)} %param.11) | copy-start | bytes 388
  51.2 8.2 %copy-start.1 = (bf16[1,1024,256]{2,1,0:T(8,128)(2,1)S(1)}, bf16[1,1024,256]{2,1,0:T(8,128)(2,1)}, u32[]{:S(2)}) copy-start(bf16[1,1024,256]{2,1,0:T(8,128)(2,1)} %param.15) | copy-start | bytes 1572868
  51.2 8.2 %copy-start.3 = (bf16[512,256]{1,0:T(8,128)(2,1)S(1)}, bf16[512,256]{1,0:T(8,128)(2,1)}, u32[]{:S(2)}) copy-start(bf16[512,256]{1,0:T(8,128)(2,1)} %param.14) | copy-start | bytes 786436
  51.4 6.3 %collective-permute-start = (bf16[2,128,256]{2,0,1:T(2,128)(2,1)S(1)}, bf16[2,128,256]{2,0,1:T(2,128)(2,1)S(1)}, u32[]{:S(2)}, u32[]{:S(2)}) collective-permute-start(bf16[2,128,256]{2,0,1:T(2,128)(2,1)S(1)} %get-tuple-element.4), channel_id=1, source_target_pairs={{0,63},{1,0},{2,1},{3,2},{4,3},{5,4},{6,5},{7,6},{8,7},{9,8},{10,9... | collective-permute-start | bytes 393224 | tf_op jit(solution)/shard_map/ppermute | solution.py:13
  53.7 5.2 %collective-permute-start.1 = (bf16[2,128,256]{2,0,1:T(2,128)(2,1)S(1)}, bf16[2,128,256]{2,0,1:T(2,128)(2,1)S(1)}, u32[]{:S(2)}, u32[]{:S(2)}) collective-permute-start(bf16[2,128,256]{2,0,1:T(2,128)(2,1)S(1)} %get-tuple-element.5), channel_id=1, source_target_pairs={{0,1},{1,2},{2,3},{3,4},{4,5},{5,6},{6,7},{7,8},{8,9},{9,10},{10,1... | collective-permute-start | bytes 393224 | tf_op jit(solution)/shard_map/ppermute | solution.py:13
  62.9 11.0 %collective-permute-start.2 = (bf16[2,128,256]{2,0,1:T(2,128)(2,1)S(1)}, bf16[2,128,256]{2,0,1:T(2,128)(2,1)S(1)}, u32[]{:S(2)}, u32[]{:S(2)}) collective-permute-start(bf16[2,128,256]{2,0,1:T(2,128)(2,1)S(1)} %copy.27), channel_id=1, source_target_pairs={{0,1},{1,2},{2,3},{3,4},{4,5},{5,6},{6,7},{7,8},{8,9},{9,10},{10,1... | collective-permute-start | bytes 393224 | tf_op jit(solution)/shard_map/ppermute | solution.py:13
  67.4 6.7 %collective-permute-start.3 = (bf16[2,128,256]{2,0,1:T(2,128)(2,1)S(1)}, bf16[2,128,256]{2,0,1:T(2,128)(2,1)S(1)}, u32[]{:S(2)}, u32[]{:S(2)}) collective-permute-start(bf16[2,128,256]{2,0,1:T(2,128)(2,1)S(1)} %copy.28), channel_id=1, source_target_pairs={{0,63},{1,0},{2,1},{3,2},{4,3},{5,4},{6,5},{7,6},{8,7},{9,8},{10,9... | collective-permute-start | bytes 393224 | tf_op jit(solution)/shard_map/ppermute | solution.py:13
  76.6 54.2 %copy-start.2 = (bf16[1,1024,256]{2,1,0:T(8,128)(2,1)S(1)}, bf16[1,1024,256]{2,1,0:T(8,128)(2,1)}, u32[]{:S(2)}) copy-start(bf16[1,1024,256]{2,1,0:T(8,128)(2,1)} %param.15) | copy-start | bytes 1572868
  120.8 18.0 %all-to-all-start.3 = ((f32[8,12,256]{2,1,0:T(8,128)}), f32[8,12,256]{2,1,0:T(8,128)S(1)}, u32[]{:S(2)}, u32[]{:S(2)}) async-start(f32[8,12,256]{2,1,0:T(8,128)} %broadcast_in_dim.42), calls=%async_computation.3 | async-start | bytes 262144 | tf_op jit(solution)/shard_map/all_to_all | solution.py:30
  138.7 25.6 %all-to-all-start.1 = ((bf16[64,16,256]{2,1,0:T(8,128)(2,1)}), bf16[64,16,256]{2,1,0:T(8,128)(2,1)S(1)}, u32[]{:S(2)}, u32[]{:S(2)}) async-start(bf16[64,16,256]{2,1,0:T(8,128)(2,1)} %bitcast.24), calls=%async_computation.1 | async-start | bytes 1048576 | tf_op jit(solution)/shard_map/all_to_all | solution.py:114
  165.4 33.7 %all-to-all-start.4 = ((f32[64,12,256]{2,1,0:T(8,128)}), f32[64,12,256]{2,1,0:T(8,128)S(1)}, u32[]{:S(2)}, u32[]{:S(2)}) async-start(f32[64,12,256]{2,1,0:T(8,128)} %broadcast_in_dim.43), calls=%async_computation.4 | async-start | bytes 2097152 | tf_op jit(solution)/shard_map/all_to_all | solution.py:30
where the time goes:
time: 202 us; the launch traced here: 201 us
  waiting for transfers between devices  65.3 us (32%)
  starting transfers between devices  50.9 us (25%)
  blocking collectives  42.1 us (21%)
  local copies, waits for them, and re-layouts  19.3 us (10%)
  matrix products  15.4 us (8%)
  other arithmetic  6.83 us (3%)
    all_to_all x1, blocking collectives, summed_on_arrival(): tiles = lax.all_to_all(split_up(x, dim, peers), axis, 0, 0, tiled=True)  42.1 us
    all_to_all x2, waiting for transfers between devices, from_everyone(): lax.all_to_all(jnp.broadcast_to(x[None], (peers, *x.shape)), axis, 0, 0,...  27.9 us
    all_to_all x1, waiting for transfers between devices, shards(): lax.all_to_all(d_nodes.reshape(ndom, per_peer, width), 'dom', split_axis=...  17.7 us
    all_to_all x1, waiting for transfers between devices, shards(): lax.all_to_all(picked, 'dom', split_axis=0, concat_axis=0, tiled=True)  17.7 us
    all_to_all x2, starting transfers between devices, from_everyone(): lax.all_to_all(jnp.broadcast_to(x[None], (peers, *x.shape)), axis, 0, 0,...  15.8 us
    ppermute x4, starting transfers between devices, passed_along(): return lax.ppermute(x, axis, [(i, (i + by) % peers) for i in range(peers)])  15.6 us
    all_to_all x1, starting transfers between devices, shards(): lax.all_to_all(picked, 'dom', split_axis=0, concat_axis=0, tiled=True)  11.6 us
    all_to_all x1, starting transfers between devices, shards(): lax.all_to_all(d_nodes.reshape(ndom, per_peer, width), 'dom', split_axis=...  7.88 us
  transfers between devices with their start and end apart: 8, of which 7 were waited for; matrix products, arithmetic and copies ran while one was open for 4% of the time, Pallas kernels for 0%

commit v1 on v0

v1 whole, which is shorter than its diff:
```python
import functools
import math

import jax
import jax.numpy as jnp
from jax import lax
from jax.experimental import pallas as pl
from jax.experimental.pallas import tpu as pltpu
from jax.sharding import PartitionSpec as P

NDOM = 64
BF = jnp.bfloat16
F32 = jnp.float32
NT = (((1,), (1,)), ((), ()))
TN = (((0,), (0,)), ((), ()))


def dot(a, b):
    return jnp.dot(a, b, preferred_element_type=F32)


def sigmoid(v):
    return jax.nn.sigmoid(v)


def rows_of(b):
    return pl.ds(pl.multiple_of(b * 128, 128), 128)


def remote(src, dst, send, recv, where):
    return pltpu.make_async_remote_copy(
        src_ref=src,
        dst_ref=dst,
        send_sem=send,
        recv_sem=recv,
        device_id=where,
        device_id_type=pl.DeviceIdType.MESH,
    )


def layer_kernel(
    feat,
    order,
    cnt,
    tgt,
    vals_hbm,
    we_hbm,
    wn_hbm,
    cot_hbm,
    node_out,
    gx_out,
    g_out,
    vals,
    we,
    wn,
    cot,
    out_rows,
    nodes,
    pre_edge,
    message,
    adj,
    adj_t,
    perm_t,
    agg,
    pre_node,
    d_node,
    d_nodes1,
    rim_out,
    rim_in,
    dwin,
    d_edge,
    back_rows,
    returned,
    in_sems,
    relay_send,
    relay_recv,
    ret_send,
    ret_recv,
    halo_send,
    halo_recv,
):
    me = lax.axis_index("dom")
    row = me // 8
    prev = lax.rem(me + NDOM - 1, NDOM)
    nxt = lax.rem(me + 1, NDOM)

    barrier = pltpu.get_barrier_semaphore()

    @pl.loop(1, NDOM)
    def _(s):
        pl.semaphore_signal(
            barrier,
            inc=1,
            device_id={"dom": lax.rem(me + s, NDOM)},
            device_id_type=pl.DeviceIdType.MESH,
        )

    loads = [
        pltpu.make_async_copy(src, dst, in_sems.at[i])
        for i, (src, dst) in enumerate(
            [(vals_hbm, vals), (we_hbm, we), (wn_hbm, wn), (cot_hbm, cot)]
        )
    ]
    for copy in loads:
        copy.start()

    def send_group(src, dst, send, recv, b):
        for jj in range(8):
            k = b * 8 + jj

            @pl.when(k != me)
            def _():
                remote(src.at[k], dst.at[me], send, recv, {"dom": k}).start()

            @pl.when(k == me)
            def _():
                pltpu.make_async_copy(src.at[k], dst.at[me], recv).start()

    far_first = [4, 3, 5, 2, 6, 1, 7, 0]

    lanes = lax.broadcasted_iota(jnp.int32, (128, 1024), 1)
    for r, shift in enumerate(far_first):
        b = lax.rem(row + shift, 8)
        own = jnp.broadcast_to(order[pl.ds(b, 1), :], (128, 128)).T
        hot = jnp.where(jnp.concatenate([own] * 8, axis=1) == lanes, 1.0, 0.0)
        picked = dot(hot.astype(BF), feat[...]).astype(BF)
        out_rows[pl.ds(pl.multiple_of(b * 8, 8), 8)] = picked.reshape(8, 16, 256)
        if r == 0:
            pl.semaphore_wait(barrier, NDOM - 1)
        send_group(out_rows, nodes, relay_send, relay_recv.at[row], b)

    down = lax.broadcasted_iota(jnp.int32, (1024, 128), 0)
    for ib in range(8):
        mine = jnp.broadcast_to(order[ib : ib + 1, :], (1024, 128))
        perm_t[:, ib * 128 : (ib + 1) * 128] = jnp.where(mine == down, 1.0, 0.0).astype(BF)
    for copy in loads:
        copy.wait()

    @pl.loop(0, 8)
    def _(c):
        blocks = []
        for s in range(4):
            live = (cnt[c] > s).astype(jnp.int32).astype(F32)
            block = vals[c, s].astype(F32) * live
            blocks.append(block)
            adj_t[c, :, s * 128 : (s + 1) * 128] = block.T.astype(BF)
        for w in range(12):
            total = None
            for s in range(4):
                hit = (tgt[c, s] == w + 6).astype(jnp.int32).astype(F32)
                term = blocks[s] * hit
                total = term if total is None else total + term
            adj[w * 128 : (w + 1) * 128, rows_of(c)] = total.astype(BF)

    for shift in reversed(far_first):
        b = lax.rem(row + shift, 8)
        group = nodes.at[pl.ds(pl.multiple_of(b * 8, 8), 8)]
        pltpu.make_async_copy(group, group, relay_recv.at[b]).wait()
        rows = group[...].reshape(128, 256)
        v = dot(rows, we[...])
        pre_edge[rows_of(b), :] = v
        message[rows_of(b), :] = (v * sigmoid(v)).astype(BF)

    rim_out[0] = dot(adj[0:256, :], message[...]).astype(BF)
    to_prev = remote(rim_out.at[0], rim_in.at[0], halo_send.at[0], halo_recv.at[0], {"dom": prev})
    to_prev.start()
    rim_out[1] = dot(adj[1280:1536, :], message[...]).astype(BF)
    to_next = remote(rim_out.at[1], rim_in.at[1], halo_send.at[1], halo_recv.at[1], {"dom": nxt})
    to_next.start()

    def flat_nodes(lo, n):
        return nodes[lo // 16 : (lo + n) // 16].reshape(n, 256)

    def node_step(lo, n):
        here = slice(lo, lo + n)
        own = flat_nodes(lo, n)
        v = pre_node[here, :] + dot(agg[here, :], wn[256:512, :])
        sig = sigmoid(v)
        node_out[here, :] = (own.astype(F32) + v * sig).astype(BF)
        g = cot[here, :].astype(F32)
        d = (g * (sig * (1.0 + v * (1.0 - sig)))).astype(BF)
        d_node[here, :] = d
        back = lax.dot_general(d, wn[...], NT, preferred_element_type=F32)
        d_nodes1[here, :] = g + back[:, :256]
        dwin[2 + lo // 128 : 2 + (lo + n) // 128] = back[:, 256:].astype(BF).reshape(n // 128, 128, 256)

    for lo in range(0, 1024, 256):
        pre_node[lo : lo + 256, :] = dot(flat_nodes(lo, 256), wn[0:256, :])
    for lo in (256, 512, 0, 768):
        agg[lo : lo + 256, :] = dot(adj[lo + 256 : lo + 512, :], message[...]).astype(BF)
    node_step(256, 512)

    to_prev.wait_recv()
    agg[768:1024, :] = (agg[768:1024, :].astype(F32) + rim_in[0].astype(F32)).astype(BF)
    node_step(768, 256)
    give_next = remote(dwin.at[8:10], dwin.at[0:2], halo_send.at[2], halo_recv.at[2], {"dom": nxt})
    give_next.start()
    to_next.wait_recv()
    agg[0:256, :] = (agg[0:256, :].astype(F32) + rim_in[1].astype(F32)).astype(BF)
    node_step(0, 256)
    give_prev = remote(dwin.at[2:4], dwin.at[10:12], halo_send.at[3], halo_recv.at[3], {"dom": prev})
    give_prev.start()

    g_out[256:512, :] = lax.dot_general(flat_nodes(0, 1024), d_node[...], TN, preferred_element_type=F32)
    g_out[512:768, :] = lax.dot_general(agg[...], d_node[...], TN, preferred_element_type=F32)
    for lo in range(0, 1024, 256):
        v = pre_edge[lo : lo + 256, :]
        sig = sigmoid(v)
        pre_edge[lo : lo + 256, :] = sig * (1.0 + v * (1.0 - sig))

    give_next.wait_recv()
    give_prev.wait_recv()
    for shift in far_first:
        c = lax.rem(row + shift, 8)
        gathered = jnp.concatenate([dwin[jnp.clip(tgt[c, s] - 6, 0, 11)] for s in range(4)], axis=0)
        dm = dot(adj_t[c], gathered).astype(BF)
        de = (dm.astype(F32) * pre_edge[rows_of(c), :]).astype(BF)
        d_edge[rows_of(c), :] = de
        dn = d_nodes1[rows_of(c), :] + lax.dot_general(de, we[...], NT, preferred_element_type=F32)
        back_rows[pl.ds(pl.multiple_of(c * 8, 8), 8)] = dn.astype(BF).reshape(8, 16, 256)
        send_group(back_rows, returned, ret_send, ret_recv, c)

    g_out[0:256, :] = lax.dot_general(flat_nodes(0, 1024), d_edge[...], TN, preferred_element_type=F32)

    pltpu.make_async_copy(returned, returned, ret_recv).wait()
    rows = returned[...].reshape(1024, 256)
    for lo in range(0, 1024, 256):
        gx_out[lo : lo + 256, :] = dot(perm_t[lo : lo + 256, :], rows).astype(BF)

    for copy in (to_prev, to_next, give_next, give_prev):
        copy.wait_send()
    others = pl.ds(0, NDOM - 1)
    for src, dst, send, recv in (
        (out_rows, nodes, relay_send, relay_recv.at[0]),
        (back_rows, returned, ret_send, ret_recv),
    ):
        remote(src.at[others], dst.at[others], send, recv, {"dom": nxt}).wait_send()


def shards(features, send_order, adj_count, adj_target, adj_vals, w_edge, w_node, cotangent):
    vmem = pl.BlockSpec(memory_space=pltpu.VMEM)
    smem = pl.BlockSpec(memory_space=pltpu.SMEM)
    hbm = pl.BlockSpec(memory_space=pl.ANY)
    V = pltpu.VMEM
    dma = pltpu.SemaphoreType.DMA
    node_out, gx, g = pl.pallas_call(
        layer_kernel,
        out_shape=(
            jax.ShapeDtypeStruct((1024, 256), BF),
            jax.ShapeDtypeStruct((1024, 256), BF),
            jax.ShapeDtypeStruct((768, 256), F32),
        ),
        in_specs=[vmem, vmem, smem, smem, hbm, hbm, hbm, hbm],
        out_specs=(vmem, vmem, vmem),
        scratch_shapes=[
            V((8, 4, 128, 128), BF),
            V((256, 256), BF),
            V((512, 256), BF),
            V((1024, 256), BF),
            V((64, 16, 256), BF),
            V((64, 16, 256), BF),
            V((1024, 256), F32),
            V((1024, 256), BF),
            V((1536, 1024), BF),
            V((8, 128, 512), BF),
            V((1024, 1024), BF),
            V((1024, 256), BF),
            V((1024, 256), F32),
            V((1024, 256), BF),
            V((1024, 256), F32),
            V((2, 256, 256), BF),
            V((2, 256, 256), BF),
            V((12, 128, 256), BF),
            V((1024, 256), BF),
            V((64, 16, 256), BF),
            V((64, 16, 256), BF),
            dma((4,)),
            dma(()),
            dma((8,)),
            dma(()),
            dma(()),
            dma((4,)),
            dma((4,)),
        ],
        compiler_params=pltpu.CompilerParams(
            collective_id=0, has_side_effects=True, vmem_limit_bytes=48 << 20
        ),
        name="layer",
    )(
        features[0],
        send_order.reshape(8, 128),
        adj_count,
        adj_target,
        adj_vals,
        w_edge,
        w_node,
        cotangent[0],
    )
    scale = 1.0 / math.sqrt(float(lax.axis_size("dp") * features.shape[1] * lax.axis_size("dom")))
    g = lax.psum(g, ("dp", "dom")) * scale
    return node_out[None], gx[None], g[:256], g[256:]


def solution(mesh):
    in_specs = (
        P("dp", "dom", None),
        P("dom", None),
        P("dom"),
        P("dom", None),
        P("dom", None, None, None),
        P(),
        P(),
        P("dp", "dom", None),
    )
    out_specs = (P("dp", "dom", None), P("dp", "dom", None), P(), P())
    return jax.shard_map(shards, mesh=mesh, in_specs=in_specs, out_specs=out_specs, check_vma=False)
```

time: 202 us -> 351 us (1.74)
  waiting for transfers between devices: 65.3 us -> 273 us
  Pallas kernels: 0 us -> 52.7 us
  starting transfers between devices: 50.9 us -> 0.04 us
  blocking collectives: 42.1 us -> 0 us
  matrix products: 15.4 us -> 0 us
  between operations: 0.93 us -> 14 us
  local copies, waits for them, and re-layouts: 19.3 us -> 9.74 us
  other arithmetic: 6.83 us -> 1.2 us
    psum x0 -> x1, waiting for transfers between devices: none -> 273 us  [shards(): g = lax.psum(g, ('dp', 'dom')) * scale]
    all_to_all x4 -> x0, waiting for transfers between devices: 63.2 us -> none  [the longest x2 27.9 us: from_everyone(): lax.all_to_all(jnp.broadcast_to(x[None], (peers, *x.shape)), axis, 0, 0,...]
    pallas_call x0 -> x1, Pallas kernels: none -> 52.7 us  [shards(): pl.pallas_call(layer_kernel, out_shape=(jax.ShapeDtypeStruct((1024, 256),...]
    all_to_all x1 -> x0, blocking collectives: 42.1 us -> none  [summed_on_arrival(): tiles = lax.all_to_all(split_up(x, dim, peers), axis, 0, 0, tiled=True)]
    all_to_all x4 -> x0, starting transfers between devices: 35.2 us -> none  [the longest x2 15.8 us: from_everyone(): lax.all_to_all(jnp.broadcast_to(x[None], (peers, *x.shape)), axis, 0, 0,...]
    ppermute x4 -> x0, starting transfers between devices: 15.6 us -> none  [passed_along(): return lax.ppermute(x, axis, [(i, (i + by) % peers) for i in range(peers)])]
    dot_general x10 -> x0, matrix products: 15.4 us -> none  [the longest x1 4.16 us: shards(): jnp.einsum('wcs,csrh->wrh', table_f, contrib, precision=lax.Precision.HIG...]
    unnamed x15 -> x17, local copies, waits for them, and re-layouts: 0.56 us -> 8.19 us
  transfers between devices with their start and end apart: 8 -> 1, of which waited for: 7 -> 1; matrix products, arithmetic and copies ran while one was open for 4% -> 0% of each run, Pallas kernels for 0% -> 0%
where the time goes in v1:
time: 351 us; the launch traced here: 350 us
  waiting for transfers between devices  273 us (78%)
  Pallas kernels  52.7 us (15%)
  between operations  14 us (4%)
  local copies, waits for them, and re-layouts  9.74 us (3%)
    psum x1, waiting for transfers between devices, shards(): g = lax.psum(g, ('dp', 'dom')) * scale  273 us
    pallas_call x1, Pallas kernels, shards(): pl.pallas_call(layer_kernel, out_shape=(jax.ShapeDtypeStruct((1024, 256),...  52.7 us
    unnamed x17, local copies, waits for them, and re-layouts  8.19 us
  transfers between devices with their start and end apart: 1, of which 1 were waited for; matrix products, arithmetic and copies ran while one was open for 0% of the time, Pallas kernels for 0%

profile of v1, /device:TPU:1, one launch (start us, length us, event | category | flops | bytes accessed | tf_op | source)
XLA Modules:
  0.0 350.3 jit_solution(2557056244660553153)
XLA Ops:
  7.2 0.0 all-reduce.2.cloned.1.call-start
  7.2 0.8 copy.12.tgt
  8.0 0.0 copy-start.5
  8.0 0.0 copy-start.6
  8.0 0.7 copy-done.5
  8.7 0.0 copy-done.6
  8.7 0.0 copy-start
  8.7 1.2 copy-done
  9.9 0.0 copy-start.1
  9.9 1.0 copy-done.1
  10.9 0.0 copy-start.2
  10.9 1.0 copy-done.2
  12.0 0.0 copy-start.3
  12.0 0.9 copy-done.3
  12.9 0.0 copy-start.4
  12.9 0.9 copy-done.4
  13.8 52.7 %layer.1 = (bf16[1024,256]{1,0:T(8,128)(2,1)S(1)}, bf16[1024,256]{1,0:T(8,128)(2,1)S(1)}, f32[768,256]{1,0:T(8,128)}) custom-call(bf16[1024,256]{1,0:T(8,128)(2,1)S(1)} %bitcast.7, s32[8,128]{1,0:T(8,128)S(1)} %bitcast.9, s32[8]{0:T(128)S(1)} %copy-done.6, s32[8,4]{1,0:T(8,128)S(1)} %copy.12.tgt, bf16[8,4,128,128]{3,2,1,0:T(8,128)(2,1)S(1)} %copy-done, ...), custom_call_target="tpu_custom_call" | custom-call | tf_op jit(solution)/shard_map/layer/pallas_call | solution.py:246
  66.5 0.0 all-reduce.2.cloned.1.call-update
  66.5 272.6 %all-reduce.2.cloned.1.call-done = f32[768,256]{1,0:T(8,128)} async-done(((f32[768,256]{1,0:T(8,128)}), f32[768,256]{1,0:T(8,128)}) %all-reduce.2.cloned.1.call-update) | async-done | bytes 786448 | tf_op jit(solution)/shard_map/psum | solution.py:300
  339.2 1.2 broadcast_multiply_fusion
  340.4 0.7 slice.8
  341.1 0.8 slice.9
  341.9 0.8 copy.16
  342.7 0.8 copy.17
Async XLA Ops:
  7.2 332.0 %all-reduce.2.cloned.1.call-start = ((), (), s32[]{:S(2)}) async-start(), calls=%async_computation | async-start | bytes 1572864 | tf_op jit(solution)/shard_map/psum | solution.py:300
  8.0 0.7 copy-start.5
  8.0 0.7 copy-start.6
  8.7 1.2 copy-start
  9.9 1.0 copy-start.1
  10.9 1.0 copy-start.2
  12.0 0.9 copy-start.3
  12.9 0.9 copy-start.4
Sparse Core Ops, SparseCore 0:
  66.6 272.4 all-reduce.1

commit v2 on v1

--- a/solution.py
+++ b/solution.py
@@ -39,7 +39,8 @@
 
 
 def layer_kernel(
-    feat,
+    scale,
+    feat_hbm,
     order,
     cnt,
     tgt,
@@ -49,7 +50,9 @@
     cot_hbm,
     node_out,
     gx_out,
-    g_out,
+    ge_out,
+    gn_out,
+    feat,
     vals,
     we,
     wn,
@@ -71,6 +74,13 @@
     d_edge,
     back_rows,
     returned,
+    part_n,
+    part_e,
+    got_n,
+    got_e,
+    sum_y,
+    sum_x,
+    whole,
     in_sems,
     relay_send,
     relay_recv,
@@ -78,8 +88,19 @@
     ret_recv,
     halo_send,
     halo_recv,
+    grad_send,
+    grad_recv,
 ):
     me = lax.axis_index("dom")
+    plane = lax.axis_index("dp")
+    core = lax.rem(me, 2)
+    col = lax.rem(me // 2, 4)
+    part = plane * 2 + core
+    parts = range(1, 16)
+
+    def member(step):
+        m = lax.rem(part + step, 16)
+        return m, {"dp": m // 2, "dom": me - core + lax.rem(m, 2)}
     row = me // 8
     prev = lax.rem(me + NDOM - 1, NDOM)
     nxt = lax.rem(me + 1, NDOM)
@@ -95,10 +116,19 @@
             device_id_type=pl.DeviceIdType.MESH,
         )
 
+    for step in range(1, 8):
+        for other in range(2):
+            pl.semaphore_signal(
+                barrier,
+                inc=1,
+                device_id={"dp": lax.rem(plane + step, 8), "dom": me - core + other},
+                device_id_type=pl.DeviceIdType.MESH,
+            )
+
     loads = [
         pltpu.make_async_copy(src, dst, in_sems.at[i])
         for i, (src, dst) in enumerate(
-            [(vals_hbm, vals), (we_hbm, we), (wn_hbm, wn), (cot_hbm, cot)]
+            [(feat_hbm, feat), (vals_hbm, vals), (we_hbm, we), (wn_hbm, wn), (cot_hbm, cot)]
         )
     ]
     for copy in loads:
@@ -116,6 +146,7 @@
             def _():
                 pltpu.make_async_copy(src.at[k], dst.at[me], recv).start()
 
+    loads[0].wait()
     far_first = [4, 3, 5, 2, 6, 1, 7, 0]
 
     lanes = lax.broadcasted_iota(jnp.int32, (128, 1024), 1)
@@ -126,14 +157,14 @@
         picked = dot(hot.astype(BF), feat[...]).astype(BF)
         out_rows[pl.ds(pl.multiple_of(b * 8, 8), 8)] = picked.reshape(8, 16, 256)
         if r == 0:
-            pl.semaphore_wait(barrier, NDOM - 1)
+            pl.semaphore_wait(barrier, NDOM - 1 + 14)
         send_group(out_rows, nodes, relay_send, relay_recv.at[row], b)
 
     down = lax.broadcasted_iota(jnp.int32, (1024, 128), 0)
     for ib in range(8):
         mine = jnp.broadcast_to(order[ib : ib + 1, :], (1024, 128))
         perm_t[:, ib * 128 : (ib + 1) * 128] = jnp.where(mine == down, 1.0, 0.0).astype(BF)
-    for copy in loads:
+    for copy in loads[1:]:
         copy.wait()
 
     @pl.loop(0, 8)
@@ -147,7 +178,7 @@
         for w in range(12):
             total = None
             for s in range(4):
-                hit = (tgt[c, s] == w + 6).astype(jnp.int32).astype(F32)
+                hit = (tgt[s, c] == w + 6).astype(jnp.int32).astype(F32)
                 term = blocks[s] * hit
                 total = term if total is None else total + term
             adj[w * 128 : (w + 1) * 128, rows_of(c)] = total.astype(BF)
@@ -201,8 +232,14 @@
     give_prev = remote(dwin.at[2:4], dwin.at[10:12], halo_send.at[3], halo_recv.at[3], {"dom": prev})
     give_prev.start()
 
-    g_out[256:512, :] = lax.dot_general(flat_nodes(0, 1024), d_node[...], TN, preferred_element_type=F32)
-    g_out[512:768, :] = lax.dot_general(agg[...], d_node[...], TN, preferred_element_type=F32)
+    top = lax.dot_general(flat_nodes(0, 1024), d_node[...], TN, preferred_element_type=F32)
+    low = lax.dot_general(agg[...], d_node[...], TN, preferred_element_type=F32)
+    part_n[0:8] = top.astype(BF).reshape(8, 32, 256)
+    part_n[8:16] = low.astype(BF).reshape(8, 32, 256)
+    got_n[part] = part_n[part]
+    for step in parts:
+        m, where = member(step)
+        remote(part_n.at[m], got_n.at[part], grad_send.at[0], grad_recv.at[0], where).start()
     for lo in range(0, 1024, 256):
         v = pre_edge[lo : lo + 256, :]
         sig = sigmoid(v)
@@ -210,23 +247,71 @@
 
     give_next.wait_recv()
     give_prev.wait_recv()
+    for c in range(8):
+        here = slice(c * 128, (c + 1) * 128)
+        gathered = jnp.concatenate([dwin[jnp.clip(tgt[s, c] - 6, 0, 11)] for s in range(4)], axis=0)
+        dm = dot(adj_t[c], gathered).astype(BF)
+        d_edge[here, :] = (dm.astype(F32) * pre_edge[here, :]).astype(BF)
+
+    edge = lax.dot_general(flat_nodes(0, 1024), d_edge[...], TN, preferred_element_type=F32)
+    part_e[...] = edge.astype(BF).reshape(16, 16, 256)
+    got_e[part] = part_e[part]
+    for step in parts:
+        m, where = member(step)
+        remote(part_e.at[m], got_e.at[part], grad_send.at[1], grad_recv.at[1], where).start()
+
     for shift in far_first:
         c = lax.rem(row + shift, 8)
-        gathered = jnp.concatenate([dwin[jnp.clip(tgt[c, s] - 6, 0, 11)] for s in range(4)], axis=0)
-        dm = dot(adj_t[c], gathered).astype(BF)
-        de = (dm.astype(F32) * pre_edge[rows_of(c), :]).astype(BF)
-        d_edge[rows_of(c), :] = de
+        de = d_edge[rows_of(c), :]
         dn = d_nodes1[rows_of(c), :] + lax.dot_general(de, we[...], NT, preferred_element_type=F32)
         back_rows[pl.ds(pl.multiple_of(c * 8, 8), 8)] = dn.astype(BF).reshape(8, 16, 256)
         send_group(back_rows, returned, ret_send, ret_recv, c)
 
-    g_out[0:256, :] = lax.dot_general(flat_nodes(0, 1024), d_edge[...], TN, preferred_element_type=F32)
+    def counted(src, dst, sems, n):
+        many = pl.ds(0, n)
+        return remote(src.at[many], dst.at[many], grad_send.at[sems], grad_recv.at[sems], {"dom": nxt})
+
+    def added(ref):
+        total = ref[0].astype(F32)
+        for i in range(1, ref.shape[0]):
+            total = total + ref[i].astype(F32)
+        return total
+
+    counted(part_n, got_n, 0, 15).wait_recv()
+    counted(part_e, got_e, 1, 15).wait_recv()
+    sum_y[row, 0:16] = added(got_e).astype(BF)
+    sum_y[row, 16:48] = added(got_n).astype(BF)
+    for step in range(1, 8):
+        other = lax.rem(row + step, 8)
+        mine = sum_y.at[row]
+        remote(mine, mine, grad_send.at[2], grad_recv.at[2], {"dom": other * 8 + lax.rem(me, 8)}).start()
+    counted(sum_y, sum_y, 2, 7).wait_recv()
+    sum_x[col] = added(sum_y).astype(BF)
+    for step in range(1, 4):
+        other = lax.rem(col + step, 4)
+        mine = sum_x.at[col]
+        remote(mine, mine, grad_send.at[3], grad_recv.at[3], {"dom": row * 8 + other * 2 + core}).start()
+    counted(sum_x, sum_x, 3, 3).wait_recv()
+    whole[part] = (added(sum_x) * scale).astype(BF)
+    for step in parts:
+        m, where = member(step)
+        mine = whole.at[part]
+        remote(mine, mine, grad_send.at[4], grad_recv.at[4], where).start()
 
     pltpu.make_async_copy(returned, returned, ret_recv).wait()
     rows = returned[...].reshape(1024, 256)
     for lo in range(0, 1024, 256):
         gx_out[lo : lo + 256, :] = dot(perm_t[lo : lo + 256, :], rows).astype(BF)
 
+    counted(whole, whole, 4, 15).wait_recv()
+    ge_out[...] = whole[:, 0:16].astype(F32).reshape(256, 256)
+    gn_out[...] = whole[:, 16:48].astype(F32).reshape(512, 256)
+
+    counted(part_n, got_n, 0, 15).wait_send()
+    counted(part_e, got_e, 1, 15).wait_send()
+    counted(sum_y, sum_y, 2, 7).wait_send()
+    counted(sum_x, sum_x, 3, 3).wait_send()
+    counted(whole, whole, 4, 15).wait_send()
     for copy in (to_prev, to_next, give_next, give_prev):
         copy.wait_send()
     others = pl.ds(0, NDOM - 1)
@@ -243,16 +328,19 @@
     hbm = pl.BlockSpec(memory_space=pl.ANY)
     V = pltpu.VMEM
     dma = pltpu.SemaphoreType.DMA
-    node_out, gx, g = pl.pallas_call(
-        layer_kernel,
+    scale = 1.0 / math.sqrt(float(lax.axis_size("dp") * features.shape[1] * lax.axis_size("dom")))
+    node_out, gx, ge, gn = pl.pallas_call(
+        functools.partial(layer_kernel, scale),
         out_shape=(
             jax.ShapeDtypeStruct((1024, 256), BF),
             jax.ShapeDtypeStruct((1024, 256), BF),
-            jax.ShapeDtypeStruct((768, 256), F32),
+            jax.ShapeDtypeStruct((256, 256), F32),
+            jax.ShapeDtypeStruct((512, 256), F32),
         ),
-        in_specs=[vmem, vmem, smem, smem, hbm, hbm, hbm, hbm],
-        out_specs=(vmem, vmem, vmem),
+        in_specs=[hbm, vmem, smem, smem, hbm, hbm, hbm, hbm],
+        out_specs=(vmem, vmem, vmem, vmem),
         scratch_shapes=[
+            V((1024, 256), BF),
             V((8, 4, 128, 128), BF),
             V((256, 256), BF),
             V((512, 256), BF),
@@ -274,31 +362,38 @@
             V((1024, 256), BF),
             V((64, 16, 256), BF),
             V((64, 16, 256), BF),
-            dma((4,)),
+            V((16, 32, 256), BF),
+            V((16, 16, 256), BF),
+            V((16, 32, 256), BF),
+            V((16, 16, 256), BF),
+            V((8, 48, 256), BF),
+            V((4, 48, 256), BF),
+            V((16, 48, 256), BF),
+            dma((5,)),
             dma(()),
             dma((8,)),
             dma(()),
             dma(()),
             dma((4,)),
             dma((4,)),
+            dma((5,)),
+            dma((5,)),
         ],
         compiler_params=pltpu.CompilerParams(
-            collective_id=0, has_side_effects=True, vmem_limit_bytes=48 << 20
+            collective_id=0, has_side_effects=True, vmem_limit_bytes=60 << 20
         ),
         name="layer",
     )(
         features[0],
         send_order.reshape(8, 128),
         adj_count,
-        adj_target,
+        adj_target.T,
         adj_vals,
         w_edge,
         w_node,
         cotangent[0],
     )
-    scale = 1.0 / math.sqrt(float(lax.axis_size("dp") * features.shape[1] * lax.axis_size("dom")))
-    g = lax.psum(g, ("dp", "dom")) * scale
-    return node_out[None], gx[None], g[:256], g[256:]
+    return node_out[None], gx[None], ge, gn
 
 
 def solution(mesh):

time: 351 us -> 82.5 us (0.24)
  waiting for transfers between devices: 273 us -> 0 us
  Pallas kernels: 52.7 us -> 76.6 us
  between operations: 14 us -> 0.65 us
  local copies, waits for them, and re-layouts: 9.74 us -> 4.95 us
    psum x1 -> x0, waiting for transfers between devices: 273 us -> none  [shards(): g = lax.psum(g, ('dp', 'dom')) * scale]
    pallas_call x1, Pallas kernels: 52.7 us -> 76.6 us  [shards(): pl.pallas_call(functools.partial(layer_kernel, scale), out_shape=(jax.Sha...]
    unnamed x17 -> x10, local copies, waits for them, and re-layouts: 8.19 us -> 4.95 us
  transfers between devices with their start and end apart: 1 -> 0, of which waited for: 1 -> 0; matrix products, arithmetic and copies ran while one was open for 0% -> 0% of each run, Pallas kernels for 0% -> 0%
where the time goes in v2:
time: 82.5 us; the launch traced here: 82.2 us
  Pallas kernels  76.6 us (93%)
  local copies, waits for them, and re-layouts  4.95 us (6%)
    pallas_call x1, Pallas kernels, shards(): pl.pallas_call(functools.partial(layer_kernel, scale), out_shape=(jax.Sha...  76.6 us
    unnamed x10, local copies, waits for them, and re-layouts  4.95 us

profile of v2, /device:TPU:1, one launch (start us, length us, event | category | flops | bytes accessed | tf_op | source)
XLA Modules:
  0.0 82.2 jit_solution(7630203517380732195)
XLA Ops:
  0.6 76.6 %layer.1 = (bf16[1024,256]{1,0:T(8,128)(2,1)}, bf16[1024,256]{1,0:T(8,128)(2,1)}, f32[256,256]{1,0:T(8,128)}, f32[512,256]{1,0:T(8,128)}) custom-call(bf16[1024,256]{1,0:T(8,128)(2,1)} %bitcast.8, s32[8,128]{1,0:T(8,128)} %bitcast.10, s32[8]{0:T(128)} %cnt.1, s32[4,8]{1,0:T(4,128)} %bitcast.11, bf16[8,4,128,128]{3,2,1,0:T(8,128)(2,1)} %vals_hbm.1, ...), custom_call_target="tpu_custom_call" | custom-call | tf_op jit(solution)/shard_map/layer/pallas_call | solution.py:332
  77.3 0.0 copy-start.1
  77.3 1.9 %copy.16 = bf16[1,1024,256]{2,1,0:T(8,128)(2,1)} copy(bf16[1,1024,256]{2,1,0:T(8,128)(2,1)} %bitcast.7) | data formatting | bytes 1048576
  79.2 0.0 copy-done.1
  79.2 0.0 copy-start.2
  79.2 0.8 copy.17
  80.0 0.3 copy-done.2
  80.3 0.0 copy-start
  80.3 0.7 copy.18
  81.0 0.4 copy-done
  81.4 0.8 copy.19
Async XLA Ops:
  77.3 1.9 %copy-start.1 = (bf16[1024,256]{1,0:T(8,128)(2,1)S(1)}, bf16[1024,256]{1,0:T(8,128)(2,1)}, u32[]{:S(2)}) copy-start(bf16[1024,256]{1,0:T(8,128)(2,1)} %get-tuple-element.9) | copy-start | bytes 1572868
  79.2 1.1 %copy-start.2 = (f32[256,256]{1,0:T(8,128)S(1)}, f32[256,256]{1,0:T(8,128)}, u32[]{:S(2)}) copy-start(f32[256,256]{1,0:T(8,128)} %get-tuple-element.18) | copy-start | bytes 786436
  80.3 1.1 %copy-start = (f32[512,256]{1,0:T(8,128)S(1)}, f32[512,256]{1,0:T(8,128)}, u32[]{:S(2)}) copy-start(f32[512,256]{1,0:T(8,128)} %get-tuple-element.19) | copy-start | bytes 1572868

commit v3 on v1

--- a/solution.py
+++ b/solution.py
@@ -39,7 +39,8 @@
 
 
 def layer_kernel(
-    feat,
+    scale,
+    feat_hbm,
     order,
     cnt,
     tgt,
@@ -47,9 +48,11 @@
     we_hbm,
     wn_hbm,
     cot_hbm,
-    node_out,
-    gx_out,
-    g_out,
+    node_hbm,
+    gx_hbm,
+    ge_hbm,
+    gn_hbm,
+    feat,
     vals,
     we,
     wn,
@@ -71,6 +74,24 @@
     d_edge,
     back_rows,
     returned,
+    node_out,
+    gx_out,
+    part_n,
+    part_e,
+    give_n,
+    give_e,
+    half_n,
+    half_e,
+    send_n,
+    send_e,
+    got_n,
+    got_e,
+    sum_yn,
+    sum_ye,
+    sum_xn,
+    sum_xe,
+    whole_n,
+    whole_e,
     in_sems,
     relay_send,
     relay_recv,
@@ -78,9 +99,16 @@
     ret_recv,
     halo_send,
     halo_recv,
+    grad_send,
+    grad_recv,
+    out_sems,
 ):
     me = lax.axis_index("dom")
+    plane = lax.axis_index("dp")
+    core = lax.rem(me, 2)
     row = me // 8
+    col = lax.rem(me // 2, 4)
+    sibling = {"dom": me + 1 - 2 * core}
     prev = lax.rem(me + NDOM - 1, NDOM)
     nxt = lax.rem(me + 1, NDOM)
 
@@ -95,18 +123,29 @@
             device_id_type=pl.DeviceIdType.MESH,
         )
 
+    for step in range(1, 8):
+        pl.semaphore_signal(
+            barrier,
+            inc=1,
+            device_id={"dp": lax.rem(plane + step, 8)},
+            device_id_type=pl.DeviceIdType.MESH,
+        )
+
     loads = [
         pltpu.make_async_copy(src, dst, in_sems.at[i])
         for i, (src, dst) in enumerate(
-            [(vals_hbm, vals), (we_hbm, we), (wn_hbm, wn), (cot_hbm, cot)]
+            [(feat_hbm, feat), (vals_hbm, vals), (we_hbm, we), (wn_hbm, wn), (cot_hbm, cot)]
         )
     ]
     for copy in loads:
         copy.start()
 
-    def send_group(src, dst, send, recv, b):
+    def send_group(src, dst, send, recv, b, shift):
         for jj in range(8):
             k = b * 8 + jj
+            if shift:
+                remote(src.at[k], dst.at[me], send, recv, {"dom": k}).start()
+                continue
 
             @pl.when(k != me)
             def _():
@@ -116,6 +155,7 @@
             def _():
                 pltpu.make_async_copy(src.at[k], dst.at[me], recv).start()
 
+    loads[0].wait()
     far_first = [4, 3, 5, 2, 6, 1, 7, 0]
 
     lanes = lax.broadcasted_iota(jnp.int32, (128, 1024), 1)
@@ -126,14 +166,14 @@
         picked = dot(hot.astype(BF), feat[...]).astype(BF)
         out_rows[pl.ds(pl.multiple_of(b * 8, 8), 8)] = picked.reshape(8, 16, 256)
         if r == 0:
-            pl.semaphore_wait(barrier, NDOM - 1)
-        send_group(out_rows, nodes, relay_send, relay_recv.at[row], b)
+            pl.semaphore_wait(barrier, NDOM - 1 + 7)
+        send_group(out_rows, nodes, relay_send, relay_recv.at[row], b, shift)
 
     down = lax.broadcasted_iota(jnp.int32, (1024, 128), 0)
     for ib in range(8):
         mine = jnp.broadcast_to(order[ib : ib + 1, :], (1024, 128))
         perm_t[:, ib * 128 : (ib + 1) * 128] = jnp.where(mine == down, 1.0, 0.0).astype(BF)
-    for copy in loads:
+    for copy in loads[1:]:
         copy.wait()
 
     @pl.loop(0, 8)
@@ -147,7 +187,7 @@
         for w in range(12):
             total = None
             for s in range(4):
-                hit = (tgt[c, s] == w + 6).astype(jnp.int32).astype(F32)
+                hit = (tgt[s, c] == w + 6).astype(jnp.int32).astype(F32)
                 term = blocks[s] * hit
                 total = term if total is None else total + term
             adj[w * 128 : (w + 1) * 128, rows_of(c)] = total.astype(BF)
@@ -201,8 +241,69 @@
     give_prev = remote(dwin.at[2:4], dwin.at[10:12], halo_send.at[3], halo_recv.at[3], {"dom": prev})
     give_prev.start()
 
-    g_out[256:512, :] = lax.dot_general(flat_nodes(0, 1024), d_node[...], TN, preferred_element_type=F32)
-    g_out[512:768, :] = lax.dot_general(agg[...], d_node[...], TN, preferred_element_type=F32)
+    outs = [pltpu.make_async_copy(node_out, node_hbm, out_sems.at[0])]
+    outs[0].start()
+
+    def counted(src, dst, i, n):
+        many = pl.ds(0, n)
+        return remote(src.at[many], dst.at[many], grad_send.at[i], grad_recv.at[i], sibling)
+
+    def swap_halves(total, part, give, half, i):
+        part[...] = total.reshape(16, -1, 256)
+        other = pl.multiple_of((1 - core) * 8, 8)
+        give[...] = part[pl.ds(other, 8)].astype(BF)
+        copy = remote(give, half, grad_send.at[i], grad_recv.at[i], sibling)
+        copy.start()
+        return copy
+
+    def over_planes(copy, part, half, send, got, i):
+        copy.wait_recv()
+        mine = part[pl.ds(pl.multiple_of(core * 8, 8), 8)]
+        send[...] = (mine + half[...].astype(F32)).astype(BF)
+        got[plane] = send[plane]
+        for step in range(1, 8):
+            z = lax.rem(plane + step, 8)
+            remote(send.at[z], got.at[plane], grad_send.at[i], grad_recv.at[i], {"dp": z}).start()
+
+    def added(ref):
+        total = ref[0].astype(F32)
+        for i in range(1, ref.shape[0]):
+            total = total + ref[i].astype(F32)
+        return total
+
+    def over_y(send, got, ring, i, j):
+        counted(send, got, i, 7).wait_recv()
+        ring[row] = added(got).astype(BF)
+        mine = ring.at[row]
+        for step in range(1, 8):
+            k = lax.rem(row + step, 8) * 8 + lax.rem(me, 8)
+            remote(mine, mine, grad_send.at[j], grad_recv.at[j], {"dom": k}).start()
+
+    def over_x(ring_y, ring, i, j):
+        counted(ring_y, ring_y, i, 7).wait_recv()
+        ring[col] = added(ring_y).astype(BF)
+        mine = ring.at[col]
+        for step in range(1, 4):
+            k = row * 8 + lax.rem(col + step, 4) * 2 + core
+            remote(mine, mine, grad_send.at[j], grad_recv.at[j], {"dom": k}).start()
+
+    def spread_planes(ring_x, whole, i, j):
+        counted(ring_x, ring_x, i, 3).wait_recv()
+        mine = whole.at[core * 8 + plane]
+        mine[...] = (added(ring_x) * scale).astype(BF)
+        for step in range(1, 8):
+            remote(mine, mine, grad_send.at[j], grad_recv.at[j], {"dp": lax.rem(plane + step, 8)}).start()
+
+    def spread_cores(whole, i, j):
+        counted(whole, whole, i, 7).wait_recv()
+        mine = whole.at[pl.ds(pl.multiple_of(core * 8, 8), 8)]
+        copy = remote(mine, mine, grad_send.at[j], grad_recv.at[j], sibling)
+        copy.start()
+        return copy
+
+    top = lax.dot_general(flat_nodes(0, 1024), d_node[...], TN, preferred_element_type=F32)
+    low = lax.dot_general(agg[...], d_node[...], TN, preferred_element_type=F32)
+    swap_n = swap_halves(jnp.concatenate([top, low], axis=0), part_n, give_n, half_n, 0)
     for lo in range(0, 1024, 256):
         v = pre_edge[lo : lo + 256, :]
         sig = sigmoid(v)
@@ -210,23 +311,63 @@
 
     give_next.wait_recv()
     give_prev.wait_recv()
-    for shift in far_first:
-        c = lax.rem(row + shift, 8)
-        gathered = jnp.concatenate([dwin[jnp.clip(tgt[c, s] - 6, 0, 11)] for s in range(4)], axis=0)
+    for c in range(8):
+        here = slice(c * 128, (c + 1) * 128)
+        gathered = jnp.concatenate([dwin[jnp.clip(tgt[s, c] - 6, 0, 11)] for s in range(4)], axis=0)
         dm = dot(adj_t[c], gathered).astype(BF)
-        de = (dm.astype(F32) * pre_edge[rows_of(c), :]).astype(BF)
-        d_edge[rows_of(c), :] = de
-        dn = d_nodes1[rows_of(c), :] + lax.dot_general(de, we[...], NT, preferred_element_type=F32)
-        back_rows[pl.ds(pl.multiple_of(c * 8, 8), 8)] = dn.astype(BF).reshape(8, 16, 256)
-        send_group(back_rows, returned, ret_send, ret_recv, c)
-
-    g_out[0:256, :] = lax.dot_general(flat_nodes(0, 1024), d_edge[...], TN, preferred_element_type=F32)
+        d_edge[here, :] = (dm.astype(F32) * pre_edge[here, :]).astype(BF)
+
+    over_planes(swap_n, part_n, half_n, send_n, got_n, 1)
+    edge = lax.dot_general(flat_nodes(0, 1024), d_edge[...], TN, preferred_element_type=F32)
+    swap_e = swap_halves(edge, part_e, give_e, half_e, 2)
+
+    def send_back(shifts):
+        for shift in shifts:
+            c = lax.rem(row + shift, 8)
+            de = d_edge[rows_of(c), :]
+            dn = d_nodes1[rows_of(c), :] + lax.dot_general(de, we[...], NT, preferred_element_type=F32)
+            back_rows[pl.ds(pl.multiple_of(c * 8, 8), 8)] = dn.astype(BF).reshape(8, 16, 256)
+            send_group(back_rows, returned, ret_send, ret_recv, c, shift)
+
+    send_back([4])
+    over_planes(swap_e, part_e, half_e, send_e, got_e, 3)
+    send_back([5])
+    over_y(send_n, got_n, sum_yn, 1, 4)
+    over_y(send_e, got_e, sum_ye, 3, 5)
+    send_back([3, 6])
+    over_x(sum_yn, sum_xn, 4, 6)
+    over_x(sum_ye, sum_xe, 5, 7)
+    send_back([2, 7, 1, 0])
+    spread_planes(sum_xn, whole_n, 6, 8)
+    spread_planes(sum_xe, whole_e, 7, 9)
+    last_n = spread_cores(whole_n, 8, 10)
 
     pltpu.make_async_copy(returned, returned, ret_recv).wait()
     rows = returned[...].reshape(1024, 256)
-    for lo in range(0, 1024, 256):
+    for i, lo in enumerate(range(0, 1024, 256)):
         gx_out[lo : lo + 256, :] = dot(perm_t[lo : lo + 256, :], rows).astype(BF)
-
+        here = pl.ds(lo, 256)
+        outs.append(pltpu.make_async_copy(gx_out.at[here], gx_hbm.at[here], out_sems.at[1 + i]))
+        outs[-1].start()
+
+    last_e = spread_cores(whole_e, 9, 11)
+    last_n.wait_recv()
+    outs.append(pltpu.make_async_copy(whole_n, gn_hbm, out_sems.at[5]))
+    outs[-1].start()
+    last_e.wait_recv()
+    outs.append(pltpu.make_async_copy(whole_e, ge_hbm, out_sems.at[6]))
+    outs[-1].start()
+
+    for copy in (swap_n, swap_e, last_n, last_e):
+        copy.wait_send()
+    counted(send_n, got_n, 1, 7).wait_send()
+    counted(send_e, got_e, 3, 7).wait_send()
+    counted(sum_yn, sum_yn, 4, 7).wait_send()
+    counted(sum_ye, sum_ye, 5, 7).wait_send()
+    counted(sum_xn, sum_xn, 6, 3).wait_send()
+    counted(sum_xe, sum_xe, 7, 3).wait_send()
+    counted(whole_n, whole_n, 8, 7).wait_send()
+    counted(whole_e, whole_e, 9, 7).wait_send()
     for copy in (to_prev, to_next, give_next, give_prev):
         copy.wait_send()
     others = pl.ds(0, NDOM - 1)
@@ -235,6 +376,62 @@
         (back_rows, returned, ret_send, ret_recv),
     ):
         remote(src.at[others], dst.at[others], send, recv, {"dom": nxt}).wait_send()
+    for copy in outs:
+        copy.wait()
+
+
+def finish_kernel(node_in, gx_in, ge_in, gn_in, node_out, gx_out, ge_out, gn_out, ge, gn, rows, grads_e, grads_n, sems):
+    loads = [
+        pltpu.make_async_copy(ge_in, ge, sems.at[0]),
+        pltpu.make_async_copy(gn_in, gn, sems.at[1]),
+    ]
+    stores = []
+    for i, (src, dst) in enumerate(((node_in, node_out), (gx_in, gx_out))):
+        for j in range(2):
+            here = pl.ds(j * 512, 512)
+            k = 2 + 2 * i + j
+            loads.append(pltpu.make_async_copy(src.at[here], rows.at[i, here], sems.at[k]))
+            stores.append(pltpu.make_async_copy(rows.at[i, here], dst.at[0, here], sems.at[4 + k]))
+    for copy in loads:
+        copy.start()
+    for load in loads[:2]:
+        load.wait()
+    for load, store in zip(loads[2:], stores):
+        load.wait()
+        store.start()
+    grads_e[...] = ge[...].astype(F32).reshape(256, 256)
+    stores.append(pltpu.make_async_copy(grads_e, ge_out, sems.at[10]))
+    stores[-1].start()
+    grads_n[...] = gn[...].astype(F32).reshape(512, 256)
+    stores.append(pltpu.make_async_copy(grads_n, gn_out, sems.at[11]))
+    stores[-1].start()
+    for store in stores:
+        store.wait()
+
+
+def finish(node_out, gx, ge, gn):
+    hbm = pl.BlockSpec(memory_space=pl.ANY)
+    return pl.pallas_call(
+        finish_kernel,
+        out_shape=(
+            jax.ShapeDtypeStruct((1, 1024, 256), BF),
+            jax.ShapeDtypeStruct((1, 1024, 256), BF),
+            jax.ShapeDtypeStruct((256, 256), F32),
+            jax.ShapeDtypeStruct((512, 256), F32),
+        ),
+        in_specs=[hbm, hbm, hbm, hbm],
+        out_specs=(hbm, hbm, hbm, hbm),
+        scratch_shapes=[
+            pltpu.VMEM((16, 16, 256), BF),
+            pltpu.VMEM((16, 32, 256), BF),
+            pltpu.VMEM((2, 1024, 256), BF),
+            pltpu.VMEM((256, 256), F32),
+            pltpu.VMEM((512, 256), F32),
+            pltpu.SemaphoreType.DMA((12,)),
+        ],
+        compiler_params=pltpu.CompilerParams(vmem_limit_bytes=60 << 20),
+        name="finish",
+    )(node_out, gx, ge, gn)
 
 
 def shards(features, send_order, adj_count, adj_target, adj_vals, w_edge, w_node, cotangent):
@@ -243,16 +440,19 @@
     hbm = pl.BlockSpec(memory_space=pl.ANY)
     V = pltpu.VMEM
     dma = pltpu.SemaphoreType.DMA
-    node_out, gx, g = pl.pallas_call(
-        layer_kernel,
+    scale = 1.0 / math.sqrt(float(lax.axis_size("dp") * features.shape[1] * lax.axis_size("dom")))
+    node_out, gx, ge, gn = pl.pallas_call(
+        functools.partial(layer_kernel, scale),
         out_shape=(
             jax.ShapeDtypeStruct((1024, 256), BF),
             jax.ShapeDtypeStruct((1024, 256), BF),
-            jax.ShapeDtypeStruct((768, 256), F32),
+            jax.ShapeDtypeStruct((16, 16, 256), BF),
+            jax.ShapeDtypeStruct((16, 32, 256), BF),
         ),
-        in_specs=[vmem, vmem, smem, smem, hbm, hbm, hbm, hbm],
-        out_specs=(vmem, vmem, vmem),
+        in_specs=[hbm, vmem, smem, smem, hbm, hbm, hbm, hbm],
+        out_specs=(hbm, hbm, hbm, hbm),
         scratch_shapes=[
+            V((1024, 256), BF),
             V((8, 4, 128, 128), BF),
             V((256, 256), BF),
             V((512, 256), BF),
@@ -274,31 +474,50 @@
             V((1024, 256), BF),
             V((64, 16, 256), BF),
             V((64, 16, 256), BF),
-            dma((4,)),
+            V((1024, 256), BF),
+            V((1024, 256), BF),
+            V((16, 32, 256), F32),
+            V((16, 16, 256), F32),
+            V((8, 32, 256), BF),
+            V((8, 16, 256), BF),
+            V((8, 32, 256), BF),
+            V((8, 16, 256), BF),
+            V((8, 32, 256), BF),
+            V((8, 16, 256), BF),
+            V((8, 32, 256), BF),
+            V((8, 16, 256), BF),
+            V((8, 32, 256), BF),
+            V((8, 16, 256), BF),
+            V((4, 32, 256), BF),
+            V((4, 16, 256), BF),
+            V((16, 32, 256), BF),
+            V((16, 16, 256), BF),
+            dma((5,)),
             dma(()),
             dma((8,)),
             dma(()),
             dma(()),
             dma((4,)),
             dma((4,)),
+            dma((12,)),
+            dma((12,)),
+            dma((7,)),
         ],
         compiler_params=pltpu.CompilerParams(
-            collective_id=0, has_side_effects=True, vmem_limit_bytes=48 << 20
+            collective_id=0, has_side_effects=True, vmem_limit_bytes=60 << 20
         ),
         name="layer",
     )(
         features[0],
         send_order.reshape(8, 128),
         adj_count,
-        adj_target,
+        adj_target.T,
         adj_vals,
         w_edge,
         w_node,
         cotangent[0],
     )
-    scale = 1.0 / math.sqrt(float(lax.axis_size("dp") * features.shape[1] * lax.axis_size("dom")))
-    g = lax.psum(g, ("dp", "dom")) * scale
-    return node_out[None], gx[None], g[:256], g[256:]
+    return finish(node_out, gx, ge, gn)
 
 
 def solution(mesh):

time: 351 us -> 72.7 us (0.21)
  waiting for transfers between devices: 273 us -> 0 us
  Pallas kernels: 52.7 us -> 71.5 us
  between operations: 14 us -> 0.64 us
  local copies, waits for them, and re-layouts: 9.74 us -> 0 us
    psum x1 -> x0, waiting for transfers between devices: 273 us -> none  [shards(): g = lax.psum(g, ('dp', 'dom')) * scale]
    pallas_call x1 -> x2, Pallas kernels: 52.7 us -> 71.5 us  [the longest x1 69 us: shards(): pl.pallas_call(functools.partial(layer_kernel, scale), out_shape=(jax.Sha...]
    unnamed x17 -> x0, local copies, waits for them, and re-layouts: 8.19 us -> none
  transfers between devices with their start and end apart: 1 -> 0, of which waited for: 1 -> 0; matrix products, arithmetic and copies ran while one was open for 0% -> 0% of each run, Pallas kernels for 0% -> 0%
where the time goes in v3:
time: 72.7 us; the launch traced here: 72.1 us
  Pallas kernels  71.5 us (98%)
    pallas_call x1, Pallas kernels, shards(): pl.pallas_call(functools.partial(layer_kernel, scale), out_shape=(jax.Sha...  69 us
    pallas_call x1, Pallas kernels, finish(): pl.pallas_call(finish_kernel, out_shape=(jax.ShapeDtypeStruct((1, 1024, 2...  2.43 us

profile of v3, /device:TPU:1, one launch (start us, length us, event | category | flops | bytes accessed | tf_op | source)
XLA Modules:
  0.0 72.1 jit_solution(12286511875055429473)
XLA Ops:
  0.6 69.0 %layer.1 = (bf16[1024,256]{1,0:T(8,128)(2,1)}, bf16[1024,256]{1,0:T(8,128)(2,1)}, bf16[16,16,256]{2,1,0:T(8,128)(2,1)}, bf16[16,32,256]{2,1,0:T(8,128)(2,1)}) custom-call(bf16[1024,256]{1,0:T(8,128)(2,1)} %bitcast.4, s32[8,128]{1,0:T(8,128)} %bitcast.6, s32[8]{0:T(128)} %cnt.1, s32[4,8]{1,0:T(4,128)} %bitcast.7, bf16[8,4,128,128]{3,2,1,0:T(8,128)(2,1)} %vals_hbm.1, ...), custom_call_target="tpu_custom_call" | custom-call | tf_op jit(solution)/shard_map/layer/pallas_call | solution.py:444
  69.7 2.4 %finish.1 = (bf16[1,1024,256]{2,1,0:T(8,128)(2,1)}, bf16[1,1024,256]{2,1,0:T(8,128)(2,1)}, f32[256,256]{1,0:T(8,128)}, f32[512,256]{1,0:T(8,128)}) custom-call(bf16[1024,256]{1,0:T(8,128)(2,1)} %get-tuple-element.8.node_in, bf16[1024,256]{1,0:T(8,128)(2,1)} %get-tuple-element.9.gx_in, bf16[16,16,256]{2,1,0:T(8,128)(2,1)} %get-tuple-element.10.ge_in, ...), custom_call_target="tpu_custom_call" | custom-call | tf_op jit(solution)/shard_map/finish/pallas_call | solution.py:414

commit v4 on v3

--- a/solution.py
+++ b/solution.py
@@ -79,16 +79,15 @@
     part_n,
     part_e,
     give_n,
-    give_e,
     half_n,
-    half_e,
     send_n,
-    send_e,
     got_n,
     got_e,
     sum_yn,
     sum_ye,
-    sum_xn,
+    send_zn,
+    got_zn,
+    all_zn,
     sum_xe,
     whole_n,
     whole_e,
@@ -124,12 +123,13 @@
         )
 
     for step in range(1, 8):
-        pl.semaphore_signal(
-            barrier,
-            inc=1,
-            device_id={"dp": lax.rem(plane + step, 8)},
-            device_id_type=pl.DeviceIdType.MESH,
-        )
+        for other in range(2):
+            pl.semaphore_signal(
+                barrier,
+                inc=1,
+                device_id={"dp": lax.rem(plane + step, 8), "dom": me - core + other},
+                device_id_type=pl.DeviceIdType.MESH,
+            )
 
     loads = [
         pltpu.make_async_copy(src, dst, in_sems.at[i])
@@ -166,7 +166,7 @@
         picked = dot(hot.astype(BF), feat[...]).astype(BF)
         out_rows[pl.ds(pl.multiple_of(b * 8, 8), 8)] = picked.reshape(8, 16, 256)
         if r == 0:
-            pl.semaphore_wait(barrier, NDOM - 1 + 7)
+            pl.semaphore_wait(barrier, NDOM - 1 + 14)
         send_group(out_rows, nodes, relay_send, relay_recv.at[row], b, shift)
 
     down = lax.broadcasted_iota(jnp.int32, (1024, 128), 0)
@@ -249,21 +249,33 @@
         return remote(src.at[many], dst.at[many], grad_send.at[i], grad_recv.at[i], sibling)
 
     def swap_halves(total, part, give, half, i):
-        part[...] = total.reshape(16, -1, 256)
-        other = pl.multiple_of((1 - core) * 8, 8)
-        give[...] = part[pl.ds(other, 8)].astype(BF)
+        part[...] = total.reshape(2, 4, 8, 8, 256)
+        give[...] = part[1 - core].astype(BF)
         copy = remote(give, half, grad_send.at[i], grad_recv.at[i], sibling)
         copy.start()
         return copy
 
-    def over_planes(copy, part, half, send, got, i):
-        copy.wait_recv()
-        mine = part[pl.ds(pl.multiple_of(core * 8, 8), 8)]
-        send[...] = (mine + half[...].astype(F32)).astype(BF)
-        got[plane] = send[plane]
-        for step in range(1, 8):
+    def to_cols(src, dst, i):
+        for step in (2, 1, 3):
+            x = lax.rem(col + step, 4)
+            k = row * 8 + x * 2 + core
+            remote(src(x), dst.at[col], grad_send.at[i], grad_recv.at[i], {"dom": k}).start()
+
+    def to_planes(src, dst, i):
+        for step in (4, 3, 5, 2, 6, 1, 7):
             z = lax.rem(plane + step, 8)
-            remote(send.at[z], got.at[plane], grad_send.at[i], grad_recv.at[i], {"dp": z}).start()
+            remote(src(z), dst.at[plane], grad_send.at[i], grad_recv.at[i], {"dp": z}).start()
+
+    part = core * 8 + plane
+
+    def to_group(src, dst, i):
+        for step in (4, 3, 5, 2, 6, 1, 7, 0):
+            for c in (core, 1 - core):
+                if step == 0 and c is core:
+                    continue
+                z = lax.rem(plane + step, 8)
+                where = {"dp": z, "dom": me - core + c} if step else sibling
+                remote(src(c * 8 + z), dst.at[part], grad_send.at[i], grad_recv.at[i], where).start()
 
     def added(ref):
         total = ref[0].astype(F32)
@@ -271,8 +283,8 @@
             total = total + ref[i].astype(F32)
         return total
 
-    def over_y(send, got, ring, i, j):
-        counted(send, got, i, 7).wait_recv()
+    def over_y(send, got, n, ring, i, j):
+        counted(send, got, i, n).wait_recv()
         ring[row] = added(got).astype(BF)
         mine = ring.at[row]
         for step in range(1, 8):
@@ -287,20 +299,6 @@
             k = row * 8 + lax.rem(col + step, 4) * 2 + core
             remote(mine, mine, grad_send.at[j], grad_recv.at[j], {"dom": k}).start()
 
-    def spread_planes(ring_x, whole, i, j):
-        counted(ring_x, ring_x, i, 3).wait_recv()
-        mine = whole.at[core * 8 + plane]
-        mine[...] = (added(ring_x) * scale).astype(BF)
-        for step in range(1, 8):
-            remote(mine, mine, grad_send.at[j], grad_recv.at[j], {"dp": lax.rem(plane + step, 8)}).start()
-
-    def spread_cores(whole, i, j):
-        counted(whole, whole, i, 7).wait_recv()
-        mine = whole.at[pl.ds(pl.multiple_of(core * 8, 8), 8)]
-        copy = remote(mine, mine, grad_send.at[j], grad_recv.at[j], sibling)
-        copy.start()
-        return copy
-
     top = lax.dot_general(flat_nodes(0, 1024), d_node[...], TN, preferred_element_type=F32)
     low = lax.dot_general(agg[...], d_node[...], TN, preferred_element_type=F32)
     swap_n = swap_halves(jnp.concatenate([top, low], axis=0), part_n, give_n, half_n, 0)
@@ -309,6 +307,11 @@
         sig = sigmoid(v)
         pre_edge[lo : lo + 256, :] = sig * (1.0 + v * (1.0 - sig))
 
+    swap_n.wait_recv()
+    send_n[...] = (part_n[core] + half_n[...].astype(F32)).astype(BF)
+    got_n[col] = send_n[col]
+    to_cols(lambda x: send_n.at[x], got_n, 1)
+
     give_next.wait_recv()
     give_prev.wait_recv()
     for c in range(8):
@@ -317,9 +320,10 @@
         dm = dot(adj_t[c], gathered).astype(BF)
         d_edge[here, :] = (dm.astype(F32) * pre_edge[here, :]).astype(BF)
 
-    over_planes(swap_n, part_n, half_n, send_n, got_n, 1)
     edge = lax.dot_general(flat_nodes(0, 1024), d_edge[...], TN, preferred_element_type=F32)
-    swap_e = swap_halves(edge, part_e, give_e, half_e, 2)
+    part_e[...] = edge.astype(BF).reshape(16, 16, 256)
+    got_e[part] = part_e[part]
+    to_group(lambda m: part_e.at[m], got_e, 3)
 
     def send_back(shifts):
         for shift in shifts:
@@ -330,17 +334,29 @@
             send_group(back_rows, returned, ret_send, ret_recv, c, shift)
 
     send_back([4])
-    over_planes(swap_e, part_e, half_e, send_e, got_e, 3)
+    counted(send_n, got_n, 1, 3).wait_recv()
+    send_zn[...] = added(got_n).astype(BF)
+    got_zn[plane] = send_zn[plane]
+    to_planes(lambda z: send_zn.at[z], got_zn, 6)
     send_back([5])
-    over_y(send_n, got_n, sum_yn, 1, 4)
-    over_y(send_e, got_e, sum_ye, 3, 5)
+    over_y(send_zn, got_zn, 7, sum_yn, 6, 4)
+    over_y(part_e, got_e, 15, sum_ye, 3, 5)
     send_back([3, 6])
-    over_x(sum_yn, sum_xn, 4, 6)
+    counted(sum_yn, sum_yn, 4, 7).wait_recv()
+    all_zn[plane] = (added(sum_yn) * scale).astype(BF)
+    to_planes(lambda z: all_zn.at[plane], all_zn, 8)
     over_x(sum_ye, sum_xe, 5, 7)
     send_back([2, 7, 1, 0])
-    spread_planes(sum_xn, whole_n, 6, 8)
-    spread_planes(sum_xe, whole_e, 7, 9)
-    last_n = spread_cores(whole_n, 8, 10)
+    counted(all_zn, all_zn, 8, 7).wait_recv()
+    mine_n = whole_n.at[core]
+    mine_n[col] = all_zn[...]
+    to_cols(lambda x: all_zn, mine_n, 11)
+    counted(sum_xe, sum_xe, 7, 3).wait_recv()
+    whole_e[part] = (added(sum_xe) * scale).astype(BF)
+    to_group(lambda m: whole_e.at[part], whole_e, 9)
+    counted(mine_n, mine_n, 11, 3).wait_recv()
+    last_n = remote(mine_n, mine_n, grad_send.at[10], grad_recv.at[10], sibling)
+    last_n.start()
 
     pltpu.make_async_copy(returned, returned, ret_recv).wait()
     rows = returned[...].reshape(1024, 256)
@@ -350,24 +366,24 @@
         outs.append(pltpu.make_async_copy(gx_out.at[here], gx_hbm.at[here], out_sems.at[1 + i]))
         outs[-1].start()
 
-    last_e = spread_cores(whole_e, 9, 11)
     last_n.wait_recv()
     outs.append(pltpu.make_async_copy(whole_n, gn_hbm, out_sems.at[5]))
     outs[-1].start()
-    last_e.wait_recv()
+    counted(whole_e, whole_e, 9, 15).wait_recv()
     outs.append(pltpu.make_async_copy(whole_e, ge_hbm, out_sems.at[6]))
     outs[-1].start()
 
-    for copy in (swap_n, swap_e, last_n, last_e):
+    for copy in (swap_n, last_n):
         copy.wait_send()
-    counted(send_n, got_n, 1, 7).wait_send()
-    counted(send_e, got_e, 3, 7).wait_send()
+    counted(send_n, got_n, 1, 3).wait_send()
+    counted(send_zn, got_zn, 6, 7).wait_send()
+    counted(all_zn, all_zn, 8, 7).wait_send()
+    counted(mine_n, mine_n, 11, 3).wait_send()
+    counted(part_e, got_e, 3, 15).wait_send()
     counted(sum_yn, sum_yn, 4, 7).wait_send()
     counted(sum_ye, sum_ye, 5, 7).wait_send()
-    counted(sum_xn, sum_xn, 6, 3).wait_send()
     counted(sum_xe, sum_xe, 7, 3).wait_send()
-    counted(whole_n, whole_n, 8, 7).wait_send()
-    counted(whole_e, whole_e, 9, 7).wait_send()
+    counted(whole_e, whole_e, 9, 15).wait_send()
     for copy in (to_prev, to_next, give_next, give_prev):
         copy.wait_send()
     others = pl.ds(0, NDOM - 1)
@@ -423,7 +439,7 @@
         out_specs=(hbm, hbm, hbm, hbm),
         scratch_shapes=[
             pltpu.VMEM((16, 16, 256), BF),
-            pltpu.VMEM((16, 32, 256), BF),
+            pltpu.VMEM((2, 4, 8, 8, 256), BF),
             pltpu.VMEM((2, 1024, 256), BF),
             pltpu.VMEM((256, 256), F32),
             pltpu.VMEM((512, 256), F32),
@@ -447,7 +463,7 @@
             jax.ShapeDtypeStruct((1024, 256), BF),
             jax.ShapeDtypeStruct((1024, 256), BF),
             jax.ShapeDtypeStruct((16, 16, 256), BF),
-            jax.ShapeDtypeStruct((16, 32, 256), BF),
+            jax.ShapeDtypeStruct((2, 4, 8, 8, 256), BF),
         ),
         in_specs=[hbm, vmem, smem, smem, hbm, hbm, hbm, hbm],
         out_specs=(hbm, hbm, hbm, hbm),
@@ -476,21 +492,20 @@
             V((64, 16, 256), BF),
             V((1024, 256), BF),
             V((1024, 256), BF),
-            V((16, 32, 256), F32),
-            V((16, 16, 256), F32),
-            V((8, 32, 256), BF),
+            V((2, 4, 8, 8, 256), F32),
+            V((16, 16, 256), BF),
+            V((4, 8, 8, 256), BF),
+            V((4, 8, 8, 256), BF),
+            V((4, 8, 8, 256), BF),
+            V((4, 8, 8, 256), BF),
+            V((16, 16, 256), BF),
+            V((8, 8, 256), BF),
             V((8, 16, 256), BF),
-            V((8, 32, 256), BF),
-            V((8, 16, 256), BF),
-            V((8, 32, 256), BF),
-            V((8, 16, 256), BF),
-            V((8, 32, 256), BF),
-            V((8, 16, 256), BF),
-            V((8, 32, 256), BF),
-            V((8, 16, 256), BF),
-            V((4, 32, 256), BF),
+            V((8, 8, 256), BF),
+            V((8, 8, 256), BF),
+            V((8, 8, 256), BF),
             V((4, 16, 256), BF),
-            V((16, 32, 256), BF),
+            V((2, 4, 8, 8, 256), BF),
             V((16, 16, 256), BF),
             dma((5,)),
             dma(()),

time: 72.7 us -> 70.8 us (0.974)
  Pallas kernels: 71.5 us -> 69.9 us
    pallas_call x1, Pallas kernels: 69 us -> 67.5 us  [shards(): pl.pallas_call(functools.partial(layer_kernel, scale), out_shape=(jax.Sha...]
where the time goes in v4:
time: 70.8 us; the launch traced here: 70.6 us
  Pallas kernels  69.9 us (99%)
    pallas_call x1, Pallas kernels, shards(): pl.pallas_call(functools.partial(layer_kernel, scale), out_shape=(jax.Sha...  67.5 us
    pallas_call x1, Pallas kernels, finish(): pl.pallas_call(finish_kernel, out_shape=(jax.ShapeDtypeStruct((1, 1024, 2...  2.43 us

profile of v4, /device:TPU:1, one launch (start us, length us, event | category | flops | bytes accessed | tf_op | source)
XLA Modules:
  0.0 70.6 jit_solution(13442159172858750735)
XLA Ops:
  0.6 67.5 %layer.1 = (bf16[1024,256]{1,0:T(8,128)(2,1)}, bf16[1024,256]{1,0:T(8,128)(2,1)}, bf16[16,16,256]{2,1,0:T(8,128)(2,1)}, bf16[2,4,8,8,256]{4,3,2,1,0:T(8,128)(2,1)}) custom-call(bf16[1024,256]{1,0:T(8,128)(2,1)} %bitcast.4, s32[8,128]{1,0:T(8,128)} %bitcast.6, s32[8]{0:T(128)} %cnt.1, s32[4,8]{1,0:T(4,128)} %bitcast.7, bf16[8,4,128,128]{3,2,1,0:T(8,128)(2,1)} %vals_hbm.1, ...), custom_call_target="tpu_custom_call" | custom-call | tf_op jit(solution)/shard_map/layer/pallas_call | solution.py:460
  68.1 2.4 %finish.1 = (bf16[1,1024,256]{2,1,0:T(8,128)(2,1)}, bf16[1,1024,256]{2,1,0:T(8,128)(2,1)}, f32[256,256]{1,0:T(8,128)}, f32[512,256]{1,0:T(8,128)}) custom-call(bf16[1024,256]{1,0:T(8,128)(2,1)} %get-tuple-element.8.node_in, bf16[1024,256]{1,0:T(8,128)(2,1)} %get-tuple-element.9.gx_in, bf16[16,16,256]{2,1,0:T(8,128)(2,1)} %get-tuple-element.10.ge_in, ...), custom_call_target="tpu_custom_call" | custom-call | tf_op jit(solution)/shard_map/finish/pallas_call | solution.py:430

commit v5 on v4

--- a/solution.py
+++ b/solution.py
@@ -111,10 +111,18 @@
     prev = lax.rem(me + NDOM - 1, NDOM)
     nxt = lax.rem(me + 1, NDOM)
 
+    loads = [
+        pltpu.make_async_copy(src, dst, in_sems.at[i])
+        for i, (src, dst) in enumerate(
+            [(feat_hbm, feat), (vals_hbm, vals), (we_hbm, we), (wn_hbm, wn), (cot_hbm, cot)]
+        )
+    ]
+    for copy in loads:
+        copy.start()
+
     barrier = pltpu.get_barrier_semaphore()
 
-    @pl.loop(1, NDOM)
-    def _(s):
+    for s in range(1, NDOM):
         pl.semaphore_signal(
             barrier,
             inc=1,
@@ -130,15 +138,6 @@
                 device_id={"dp": lax.rem(plane + step, 8), "dom": me - core + other},
                 device_id_type=pl.DeviceIdType.MESH,
             )
-
-    loads = [
-        pltpu.make_async_copy(src, dst, in_sems.at[i])
-        for i, (src, dst) in enumerate(
-            [(feat_hbm, feat), (vals_hbm, vals), (we_hbm, we), (wn_hbm, wn), (cot_hbm, cot)]
-        )
-    ]
-    for copy in loads:
-        copy.start()
 
     def send_group(src, dst, send, recv, b, shift):
         for jj in range(8):
@@ -340,19 +339,21 @@
     to_planes(lambda z: send_zn.at[z], got_zn, 6)
     send_back([5])
     over_y(send_zn, got_zn, 7, sum_yn, 6, 4)
-    over_y(part_e, got_e, 15, sum_ye, 3, 5)
+    counted(part_e, got_e, 3, 15).wait_recv()
+    sum_xe[col] = added(got_e).astype(BF)
+    to_cols(lambda x: sum_xe.at[col], sum_xe, 7)
     send_back([3, 6])
     counted(sum_yn, sum_yn, 4, 7).wait_recv()
     all_zn[plane] = (added(sum_yn) * scale).astype(BF)
     to_planes(lambda z: all_zn.at[plane], all_zn, 8)
-    over_x(sum_ye, sum_xe, 5, 7)
+    over_y(sum_xe, sum_xe, 3, sum_ye, 7, 5)
     send_back([2, 7, 1, 0])
     counted(all_zn, all_zn, 8, 7).wait_recv()
     mine_n = whole_n.at[core]
     mine_n[col] = all_zn[...]
     to_cols(lambda x: all_zn, mine_n, 11)
-    counted(sum_xe, sum_xe, 7, 3).wait_recv()
-    whole_e[part] = (added(sum_xe) * scale).astype(BF)
+    counted(sum_ye, sum_ye, 5, 7).wait_recv()
+    whole_e[part] = (added(sum_ye) * scale).astype(BF)
     to_group(lambda m: whole_e.at[part], whole_e, 9)
     counted(mine_n, mine_n, 11, 3).wait_recv()
     last_n = remote(mine_n, mine_n, grad_send.at[10], grad_recv.at[10], sibling)

time: 70.8 us -> 70.4 us (level)
  no operation moved by 1% of the time
where the time goes in v5:
time: 70.4 us; the launch traced here: 70.2 us
  Pallas kernels  69.5 us (99%)
    pallas_call x1, Pallas kernels, shards(): pl.pallas_call(functools.partial(layer_kernel, scale), out_shape=(jax.Sha...  67.1 us
    pallas_call x1, Pallas kernels, finish(): pl.pallas_call(finish_kernel, out_shape=(jax.ShapeDtypeStruct((1, 1024, 2...  2.43 us

profile of v5, /device:TPU:1, one launch (start us, length us, event | category | flops | bytes accessed | tf_op | source)
XLA Modules:
  0.0 70.2 jit_solution(861415785709534405)
XLA Ops:
  0.6 67.1 %layer.1 = (bf16[1024,256]{1,0:T(8,128)(2,1)}, bf16[1024,256]{1,0:T(8,128)(2,1)}, bf16[16,16,256]{2,1,0:T(8,128)(2,1)}, bf16[2,4,8,8,256]{4,3,2,1,0:T(8,128)(2,1)}) custom-call(bf16[1024,256]{1,0:T(8,128)(2,1)} %bitcast.4, s32[8,128]{1,0:T(8,128)} %bitcast.6, s32[8]{0:T(128)} %cnt.1, s32[4,8]{1,0:T(4,128)} %bitcast.7, bf16[8,4,128,128]{3,2,1,0:T(8,128)(2,1)} %vals_hbm.1, ...), custom_call_target="tpu_custom_call" | custom-call | tf_op jit(solution)/shard_map/layer/pallas_call | solution.py:461
  67.7 2.4 %finish.1 = (bf16[1,1024,256]{2,1,0:T(8,128)(2,1)}, bf16[1,1024,256]{2,1,0:T(8,128)(2,1)}, f32[256,256]{1,0:T(8,128)}, f32[512,256]{1,0:T(8,128)}) custom-call(bf16[1024,256]{1,0:T(8,128)(2,1)} %get-tuple-element.8.node_in, bf16[1024,256]{1,0:T(8,128)(2,1)} %get-tuple-element.9.gx_in, bf16[16,16,256]{2,1,0:T(8,128)(2,1)} %get-tuple-element.10.ge_in, ...), custom_call_target="tpu_custom_call" | custom-call | tf_op jit(solution)/shard_map/finish/pallas_call | solution.py:431

commit v6 on v5

--- a/solution.py
+++ b/solution.py
@@ -349,16 +349,17 @@
     over_y(sum_xe, sum_xe, 3, sum_ye, 7, 5)
     send_back([2, 7, 1, 0])
     counted(all_zn, all_zn, 8, 7).wait_recv()
-    mine_n = whole_n.at[core]
-    mine_n[col] = all_zn[...]
-    to_cols(lambda x: all_zn, mine_n, 11)
+    mine_n = core * 4 + col
+    whole_n[mine_n] = all_zn[...]
+    for step in (2, 1, 3, 0):
+        for c in (core, 1 - core):
+            if step == 0 and c is core:
+                continue
+            k = row * 8 + lax.rem(col + step, 4) * 2 + c
+            remote(all_zn, whole_n.at[mine_n], grad_send.at[11], grad_recv.at[11], {"dom": k}).start()
     counted(sum_ye, sum_ye, 5, 7).wait_recv()
     whole_e[part] = (added(sum_ye) * scale).astype(BF)
     to_group(lambda m: whole_e.at[part], whole_e, 9)
-    counted(mine_n, mine_n, 11, 3).wait_recv()
-    last_n = remote(mine_n, mine_n, grad_send.at[10], grad_recv.at[10], sibling)
-    last_n.start()
-
     pltpu.make_async_copy(returned, returned, ret_recv).wait()
     rows = returned[...].reshape(1024, 256)
     for i, lo in enumerate(range(0, 1024, 256)):
@@ -367,19 +368,18 @@
         outs.append(pltpu.make_async_copy(gx_out.at[here], gx_hbm.at[here], out_sems.at[1 + i]))
         outs[-1].start()
 
-    last_n.wait_recv()
+    counted(whole_n, whole_n, 11, 7).wait_recv()
     outs.append(pltpu.make_async_copy(whole_n, gn_hbm, out_sems.at[5]))
     outs[-1].start()
     counted(whole_e, whole_e, 9, 15).wait_recv()
     outs.append(pltpu.make_async_copy(whole_e, ge_hbm, out_sems.at[6]))
     outs[-1].start()
 
-    for copy in (swap_n, last_n):
-        copy.wait_send()
+    swap_n.wait_send()
     counted(send_n, got_n, 1, 3).wait_send()
     counted(send_zn, got_zn, 6, 7).wait_send()
     counted(all_zn, all_zn, 8, 7).wait_send()
-    counted(mine_n, mine_n, 11, 3).wait_send()
+    counted(whole_n, whole_n, 11, 7).wait_send()
     counted(part_e, got_e, 3, 15).wait_send()
     counted(sum_yn, sum_yn, 4, 7).wait_send()
     counted(sum_ye, sum_ye, 5, 7).wait_send()
@@ -440,7 +440,7 @@
         out_specs=(hbm, hbm, hbm, hbm),
         scratch_shapes=[
             pltpu.VMEM((16, 16, 256), BF),
-            pltpu.VMEM((2, 4, 8, 8, 256), BF),
+            pltpu.VMEM((8, 8, 8, 256), BF),
             pltpu.VMEM((2, 1024, 256), BF),
             pltpu.VMEM((256, 256), F32),
             pltpu.VMEM((512, 256), F32),
@@ -464,7 +464,7 @@
             jax.ShapeDtypeStruct((1024, 256), BF),
             jax.ShapeDtypeStruct((1024, 256), BF),
             jax.ShapeDtypeStruct((16, 16, 256), BF),
-            jax.ShapeDtypeStruct((2, 4, 8, 8, 256), BF),
+            jax.ShapeDtypeStruct((8, 8, 8, 256), BF),
         ),
         in_specs=[hbm, vmem, smem, smem, hbm, hbm, hbm, hbm],
         out_specs=(hbm, hbm, hbm, hbm),
@@ -506,7 +506,7 @@
             V((8, 8, 256), BF),
             V((8, 8, 256), BF),
             V((4, 16, 256), BF),
-            V((2, 4, 8, 8, 256), BF),
+            V((8, 8, 8, 256), BF),
             V((16, 16, 256), BF),
             dma((5,)),
             dma(()),

time: 70.4 us -> 70.4 us (level)
  no operation moved by 1% of the time
where the time goes in v6:
time: 70.4 us; the launch traced here: 70.2 us
  Pallas kernels  69.5 us (99%)
    pallas_call x1, Pallas kernels, shards(): pl.pallas_call(functools.partial(layer_kernel, scale), out_shape=(jax.Sha...  67.1 us
    pallas_call x1, Pallas kernels, finish(): pl.pallas_call(finish_kernel, out_shape=(jax.ShapeDtypeStruct((1, 1024, 2...  2.43 us

profile of v6, /device:TPU:1, one launch (start us, length us, event | category | flops | bytes accessed | tf_op | source)
XLA Modules:
  0.0 70.2 jit_solution(13379506969025014731)
XLA Ops:
  0.6 67.1 %layer.1 = (bf16[1024,256]{1,0:T(8,128)(2,1)}, bf16[1024,256]{1,0:T(8,128)(2,1)}, bf16[16,16,256]{2,1,0:T(8,128)(2,1)}, bf16[8,8,8,256]{3,2,1,0:T(8,128)(2,1)}) custom-call(bf16[1024,256]{1,0:T(8,128)(2,1)} %bitcast.4, s32[8,128]{1,0:T(8,128)} %bitcast.6, s32[8]{0:T(128)} %cnt.1, s32[4,8]{1,0:T(4,128)} %bitcast.7, bf16[8,4,128,128]{3,2,1,0:T(8,128)(2,1)} %vals_hbm.1, ...), custom_call_target="tpu_custom_call" | custom-call | tf_op jit(solution)/shard_map/layer/pallas_call | solution.py:461
  67.7 2.4 %finish.1 = (bf16[1,1024,256]{2,1,0:T(8,128)(2,1)}, bf16[1,1024,256]{2,1,0:T(8,128)(2,1)}, f32[256,256]{1,0:T(8,128)}, f32[512,256]{1,0:T(8,128)}) custom-call(bf16[1024,256]{1,0:T(8,128)(2,1)} %get-tuple-element.8.node_in, bf16[1024,256]{1,0:T(8,128)(2,1)} %get-tuple-element.9.gx_in, bf16[16,16,256]{2,1,0:T(8,128)(2,1)} %get-tuple-element.10.ge_in, ...), custom_call_target="tpu_custom_call" | custom-call | tf_op jit(solution)/shard_map/finish/pallas_call | solution.py:431
